TPU v7x, 32 devices: a whole 2x2x4 slice. The times are simulated.
32 devices in a mesh: groups: 2 (over y), ctx: 16 (over z, x, core).
Axes of the slice: x: 2, y: 2, z: 4, core: 2. Of those that a mesh axis runs over, the one named last changes fastest.
Arguments:
- queries: bfloat16 [8192, 8192], P(('groups', 'ctx')), parts along dimension 0, may hold values from -10 to 10
- keys: bfloat16 [8192, 1024], P(('groups', 'ctx')), parts along dimension 0, may hold values from -6 to 6
- values: bfloat16 [8192, 1024], P(('groups', 'ctx')), parts along dimension 0, may hold values from -6 to 6
- positions: int32 [8192], P(('groups', 'ctx')), parts along dimension 0, may hold values from 0 to 4096, as said below
- picks: int32 [64, 8, 2], P(('groups', 'ctx')), parts along dimension 0, may hold values from -1 to 31, as said below
Outputs:
- attended: bfloat16 [8192, 8192], P(('groups', 'ctx')), parts along dimension 0
There are 2 independent parts, one for each index of `groups`. A program takes and returns all parts, laid end to end along the dimension named above; each array names one. Nothing has to cross between parts.
Inputs may be any that keep to these rules, and one draw needn't show every extreme that they name: positions never fall from one token to the next and each lies in [index, index + 1]; the first is 0 and the last is 4096. A pick of query block b is -1 or a block held by an earlier shard, so its index is below (b // 2) * 2; it may lie inside the band, and then its keys count twice; the two picks of one query block and head differ when both are set, and both are set or both -1; over the 2 query blocks of one shard and all heads, at most 2 picks name blocks of one shard, and some shard has exactly 2 for some other shard in every draw.
All inputs are finite; a program needn't handle non-finite values.
Results may differ from a plain program's by a relative error of at most 0.009.
Values may be sent and summed in bfloat16 or wider, within the bound.
No kernel may reach another device: no remote copies, remote signals or barrier semaphores. Data moves between devices by JAX's collectives and lax.ppermute only.
A program may use at most 192 MiB of HBM per device.

v0:
```python
import functools

import jax
import jax.numpy as jnp
from jax import lax
from jax.experimental import pallas as pl
from jax.experimental.pallas import tpu as pltpu
from jax.sharding import PartitionSpec as P

QUERY_HEADS = 64
KEY_VALUE_HEADS = 8
HEAD_SIZE = 128
BLOCK_TOKENS = 128
LOCAL_BAND_SIZE = 4
PICKED_BLOCKS = 2
GROUP = QUERY_HEADS // KEY_VALUE_HEADS
ROWS = GROUP * BLOCK_TOKENS
PAIR = 2 * HEAD_SIZE
BLOCKS = 2

rope_base = 500000.0
masked_score = -1e30
score_factor = HEAD_SIZE ** (-0.5) * 1.4426950408889634

BAND_ROWS = 256
PICK_ROWS = 256

SMEM = pltpu.MemorySpace.SMEM


def from_behind(block, axis, distance):
    devices = range(lax.axis_size(axis))
    route = [(i - distance, i) for i in devices if i - distance in devices]
    return lax.ppermute(block, axis, route)


def rotary_tables(pos):
    half = HEAD_SIZE // 2
    freq = rope_base ** (-(jnp.arange(half, dtype=jnp.float32) * 2.0) / HEAD_SIZE)
    angle = pos.astype(jnp.float32)[:, None] * freq[None, :]
    cosine = jnp.cos(angle)
    sine = jnp.sin(angle)
    return jnp.concatenate([cosine, cosine], -1), jnp.concatenate([-sine, sine], -1)


def rotate(x, cosine, sine):
    wide = x.astype(jnp.float32)
    swapped = pltpu.roll(wide, HEAD_SIZE // 2, 1)
    return (wide * cosine + swapped * sine).astype(jnp.bfloat16)


def prep_kernel(limit, picks_ref, k_ref, v_ref, cos_ref, sin_ref, kv_ref, last_ref, table_ref, slot_ref, count_ref):
    shards = table_ref.shape[0]

    @pl.loop(0, shards)
    def _(i):
        count_ref[i] = 0
        for r in range(limit):
            table_ref[i, r] = -1

    @pl.loop(0, BLOCKS * KEY_VALUE_HEADS)
    def _(i):
        b = i // KEY_VALUE_HEADS
        h = i % KEY_VALUE_HEADS
        for p in range(PICKED_BLOCKS):
            pick = picks_ref[b, h, p]
            slot_ref[i, p] = -1

            @pl.when(pick >= 0)
            def _():
                owner = pick // BLOCKS
                rank = jnp.minimum(count_ref[owner], limit - 1)
                count_ref[owner] = rank + 1
                table_ref[owner, rank] = pick % BLOCKS * KEY_VALUE_HEADS + h
                slot_ref[i, p] = owner * limit + rank

    for b in range(BLOCKS):
        rows = slice(b * BLOCK_TOKENS, (b + 1) * BLOCK_TOKENS)
        cosine = cos_ref[rows, :]
        sine = sin_ref[rows, :]
        for h in range(KEY_VALUE_HEADS):
            cols = slice(h * HEAD_SIZE, (h + 1) * HEAD_SIZE)
            rotated = rotate(k_ref[rows, cols], cosine, sine)
            value = v_ref[rows, cols]
            kv_ref[b, h, :, :HEAD_SIZE] = rotated
            kv_ref[b, h, :, HEAD_SIZE:] = value
            if b == BLOCKS - 1:
                last_ref[0, h, :, :HEAD_SIZE] = rotated
                last_ref[0, h, :, HEAD_SIZE:] = value


def gather_kernel(wanted_ref, kv_ref, out_ref, sems):
    shards, limit = wanted_ref.shape

    def copy(i, r):
        entry = jnp.maximum(wanted_ref[i, r], 0)
        return pltpu.make_async_copy(
            kv_ref.at[entry // KEY_VALUE_HEADS, entry % KEY_VALUE_HEADS],
            out_ref.at[i, r],
            sems.at[i, r],
        )

    @pl.loop(0, shards)
    def _(i):
        for r in range(limit):
            copy(i, r).start()

    @pl.loop(0, shards)
    def _(i):
        for r in range(limit):
            copy(i, r).wait()


def scores_of(query, key):
    return lax.dot_general(query, key, (((1,), (1,)), ((), ())), preferred_element_type=jnp.float32)


def summed(weight, value):
    both = jnp.concatenate([value, jnp.ones_like(value)], 1)
    out = jnp.dot(weight, both, preferred_element_type=jnp.float32)
    return out[:, :HEAD_SIZE], out[:, HEAD_SIZE:]


def band_kernel(me_ref, q_ref, cos_ref, sin_ref, far_ref, near_ref, own_ref, qr_ref, acc_ref, stat_ref):
    me = me_ref[0]
    row = lax.broadcasted_iota(jnp.int32, (BLOCK_TOKENS, BLOCK_TOKENS), 0)
    col = lax.broadcasted_iota(jnp.int32, (BLOCK_TOKENS, BLOCK_TOKENS), 1)
    causal = jnp.concatenate([col <= row] * (BAND_ROWS // BLOCK_TOKENS), 0)
    lane = lax.broadcasted_iota(jnp.int32, (BLOCK_TOKENS, HEAD_SIZE), 1)

    for b in range(BLOCKS):
        rows = slice(b * BLOCK_TOKENS, (b + 1) * BLOCK_TOKENS)
        for g in range(GROUP):
            qr_ref[b, 0, g * BLOCK_TOKENS : (g + 1) * BLOCK_TOKENS, :] = rotate(
                q_ref[rows, g * HEAD_SIZE : (g + 1) * HEAD_SIZE], cos_ref[rows, :], sin_ref[rows, :]
            )

    def attend(start):
        for b in range(BLOCKS):
            pieces = [far_ref[0, 0], near_ref[0, 0], near_ref[1, 0], own_ref[0, 0], own_ref[1, 0]]
            window = jnp.concatenate(pieces[b : b + LOCAL_BAND_SIZE], 0)
            key = window[:, :HEAD_SIZE]
            value = window[:, HEAD_SIZE:]
            stat = jnp.zeros((BLOCK_TOKENS, HEAD_SIZE), jnp.float32)
            for first in range(0, ROWS, BAND_ROWS):
                part = slice(first, first + BAND_ROWS)
                score = scores_of(qr_ref[b, 0, part, :], key)
                edge = (LOCAL_BAND_SIZE - 1) * BLOCK_TOKENS
                before = score[:, :edge]
                if start:
                    oldest = (me * BLOCKS + b - (LOCAL_BAND_SIZE - 1)) * BLOCK_TOKENS
                    index = oldest + lax.broadcasted_iota(jnp.int32, before.shape, 1)
                    before = jnp.where(index >= 0, before, masked_score)
                score = jnp.concatenate([before, jnp.where(causal, score[:, edge:], masked_score)], 1)
                top = jnp.max(score, -1, keepdims=True) * score_factor
                weight = jnp.exp2(score * score_factor - top)
                out, total = summed(weight.astype(jnp.bfloat16), value)
                acc_ref[b, 0, part, :] = out.astype(acc_ref.dtype)
                for g in range(BAND_ROWS // BLOCK_TOKENS):
                    at = slice(g * BLOCK_TOKENS, (g + 1) * BLOCK_TOKENS)
                    head = first // BLOCK_TOKENS + g
                    stat = jnp.where(lane == head, top[at], stat)
                    stat = jnp.where(lane == GROUP + head, total[at], stat)
            stat_ref[b, 0] = stat

    early = me * BLOCKS < LOCAL_BAND_SIZE - 1

    @pl.when(early)
    def _():
        attend(True)

    @pl.when(jnp.logical_not(early))
    def _():
        attend(False)


def picks_kernel(slot_ref, q_ref, first_ref, second_ref, acc_ref, stat_ref, out_ref):
    live = slot_ref[pl.program_id(0), 0] >= 0

    def column(ref_value, at):
        return ref_value[:, at : at + 1]

    @pl.when(live)
    def _():
        window = jnp.concatenate([first_ref[0], second_ref[0]], 0)
        key = window[:, :HEAD_SIZE]
        value = window[:, HEAD_SIZE:]
        stat = stat_ref[0, 0]
        for first in range(0, ROWS, PICK_ROWS):
            part = slice(first, first + PICK_ROWS)
            heads = range(first // BLOCK_TOKENS, (first + PICK_ROWS) // BLOCK_TOKENS)
            score = scores_of(q_ref[0, 0, part, :], key)
            old_top = jnp.concatenate([column(stat, g) for g in heads], 0)
            old_total = jnp.concatenate([column(stat, GROUP + g) for g in heads], 0)
            top = jnp.maximum(jnp.max(score, -1, keepdims=True) * score_factor, old_top)
            weight = jnp.exp2(score * score_factor - top)
            fade = jnp.exp2(old_top - top)
            out, total = summed(weight.astype(jnp.bfloat16), value)
            out = out + acc_ref[0, 0, part, :].astype(jnp.float32) * fade
            result = (out / (total + old_total * fade)).astype(out_ref.dtype)
            for g in heads:
                at = slice(g * BLOCK_TOKENS - first, (g + 1) * BLOCK_TOKENS - first)
                out_ref[:, g * HEAD_SIZE : (g + 1) * HEAD_SIZE] = result[at]

    @pl.when(jnp.logical_not(live))
    def _():
        stat = stat_ref[0, 0]
        for g in range(GROUP):
            acc = acc_ref[0, 0, g * BLOCK_TOKENS : (g + 1) * BLOCK_TOKENS, :].astype(jnp.float32)
            out_ref[:, g * HEAD_SIZE : (g + 1) * HEAD_SIZE] = (acc / column(stat, GROUP + g)).astype(out_ref.dtype)


def shards(queries, keys, values, positions, picks):
    tokens = queries.shape[0]
    window = lax.axis_size("ctx")
    limit = max(1, BLOCKS * KEY_VALUE_HEADS * PICKED_BLOCKS // window)
    me = lax.axis_index("ctx").astype(jnp.int32).reshape(1)
    cosine, sine = rotary_tables(positions)
    bf16 = jnp.bfloat16
    vmem = pl.BlockSpec(memory_space=pltpu.MemorySpace.VMEM)
    smem = pl.BlockSpec(memory_space=SMEM)
    hbm = pl.BlockSpec(memory_space=pl.ANY)

    kv, last, table, slot = pl.pallas_call(
        functools.partial(prep_kernel, limit),
        out_shape=(
            jax.ShapeDtypeStruct((BLOCKS, KEY_VALUE_HEADS, BLOCK_TOKENS, PAIR), bf16),
            jax.ShapeDtypeStruct((1, KEY_VALUE_HEADS, BLOCK_TOKENS, PAIR), bf16),
            jax.ShapeDtypeStruct((window, limit), jnp.int32),
            jax.ShapeDtypeStruct((BLOCKS * KEY_VALUE_HEADS, PICKED_BLOCKS), jnp.int32),
        ),
        in_specs=[smem, vmem, vmem, vmem, vmem],
        out_specs=(vmem, vmem, smem, smem),
        scratch_shapes=[pltpu.SMEM((window,), jnp.int32)],
        name="prep",
    )(picks, keys, values, cosine, sine)

    near = from_behind(kv, "ctx", 1)
    far = from_behind(last, "ctx", 2)
    wanted = lax.all_to_all(table, "ctx", split_axis=0, concat_axis=0, tiled=True)

    answer = pl.pallas_call(
        gather_kernel,
        out_shape=jax.ShapeDtypeStruct((window, limit, BLOCK_TOKENS, PAIR), bf16),
        in_specs=[smem, hbm],
        out_specs=hbm,
        scratch_shapes=[pltpu.SemaphoreType.DMA((window, limit))],
        name="gather",
    )(wanted, kv)
    landed = lax.all_to_all(answer, "ctx", split_axis=0, concat_axis=0, tiled=True)
    landed = landed.reshape(window * limit, BLOCK_TOKENS, PAIR)

    per_head = lambda *shape: pl.BlockSpec((shape[0], 1) + shape[1:], lambda h, *_: (0, h, 0, 0))
    band_flops = 4 * BLOCKS * QUERY_HEADS * BLOCK_TOKENS * LOCAL_BAND_SIZE * BLOCK_TOKENS * HEAD_SIZE
    rotated, acc, stat = pl.pallas_call(
        band_kernel,
        out_shape=(
            jax.ShapeDtypeStruct((BLOCKS, KEY_VALUE_HEADS, ROWS, HEAD_SIZE), bf16),
            jax.ShapeDtypeStruct((BLOCKS, KEY_VALUE_HEADS, ROWS, HEAD_SIZE), bf16),
            jax.ShapeDtypeStruct((BLOCKS, KEY_VALUE_HEADS, BLOCK_TOKENS, HEAD_SIZE), jnp.float32),
        ),
        grid_spec=pltpu.PrefetchScalarGridSpec(
            num_scalar_prefetch=1,
            grid=(KEY_VALUE_HEADS,),
            in_specs=[
                pl.BlockSpec((tokens, ROWS), lambda h, *_: (0, h)),
                pl.BlockSpec((tokens, HEAD_SIZE), lambda h, *_: (0, 0)),
                pl.BlockSpec((tokens, HEAD_SIZE), lambda h, *_: (0, 0)),
                per_head(1, BLOCK_TOKENS, PAIR),
                per_head(BLOCKS, BLOCK_TOKENS, PAIR),
                per_head(BLOCKS, BLOCK_TOKENS, PAIR),
            ],
            out_specs=(
                per_head(BLOCKS, ROWS, HEAD_SIZE),
                per_head(BLOCKS, ROWS, HEAD_SIZE),
                per_head(BLOCKS, BLOCK_TOKENS, HEAD_SIZE),
            ),
        ),
        cost_estimate=pl.CostEstimate(flops=4 * band_flops, bytes_accessed=16 << 20, transcendentals=1 << 23),
        compiler_params=pltpu.CompilerParams(vmem_limit_bytes=32 << 20),
        name="band",
    )(me, queries, cosine, sine, far, near, kv)

    at_slot = lambda p: pl.BlockSpec(
        (1, BLOCK_TOKENS, PAIR), lambda i, slots: (jnp.maximum(slots[i, p], 0), 0, 0)
    )
    per_pair = lambda *shape: pl.BlockSpec(
        (1, 1) + shape, lambda i, *_: (i // KEY_VALUE_HEADS, i % KEY_VALUE_HEADS, 0, 0)
    )
    return pl.pallas_call(
        picks_kernel,
        out_shape=jax.ShapeDtypeStruct((tokens, QUERY_HEADS * HEAD_SIZE), bf16),
        grid_spec=pltpu.PrefetchScalarGridSpec(
            num_scalar_prefetch=1,
            grid=(BLOCKS * KEY_VALUE_HEADS,),
            in_specs=[
                per_pair(ROWS, HEAD_SIZE),
                at_slot(0),
                at_slot(1),
                per_pair(ROWS, HEAD_SIZE),
                per_pair(BLOCK_TOKENS, HEAD_SIZE),
            ],
            out_specs=pl.BlockSpec((BLOCK_TOKENS, ROWS), lambda i, *_: (i // KEY_VALUE_HEADS, i % KEY_VALUE_HEADS)),
        ),
        cost_estimate=pl.CostEstimate(flops=2 * band_flops, bytes_accessed=16 << 20, transcendentals=1 << 22),
        compiler_params=pltpu.CompilerParams(vmem_limit_bytes=32 << 20),
        name="picks",
    )(slot, rotated, landed, landed, acc, stat)


def solution(mesh):
    return jax.shard_map(
        shards,
        mesh=mesh,
        in_specs=(
            P(("groups", "ctx"), None),
            P(("groups", "ctx"), None),
            P(("groups", "ctx"), None),
            P(("groups", "ctx")),
            P(("groups", "ctx"), None, None),
        ),
        out_specs=P(("groups", "ctx"), None),
        check_vma=False,
    )
```

profile of v0, /device:TPU:17, one launch (start us, length us, event | category | flops | bytes accessed | tf_op | source)
XLA Modules:
  0.0 208.3 jit_solution(10555860271264194020)
XLA Ops:
  0.0 0.7 convert_element_type.3
  0.7 1.4 copy.9.picks_ref
  2.1 0.5 fusion
  2.6 0.8 pad_maximum_fusion
  3.4 0.0 copy-start.1
  3.4 0.0 copy-start.2
  3.4 3.5 %prep.1 = (bf16[2,8,128,256]{3,2,1,0:T(8,128)(2,1)}, bf16[1,8,128,256]{3,2,1,0:T(8,128)(2,1)}, s32[16,2]{1,0:T(8,128)}, s32[16,2]{1,0:T(8,128)}) custom-call(s32[2,8,2]{2,1,0:T(8,128)} %copy.9.picks_ref, bf16[256,1024]{1,0:T(8,128)(2,1)} %k_ref.1, bf16[256,1024]{1,0:T(8,128)(2,1)} %v_ref.1, f32[256,128]{1,0:T(8,128)} %get-tuple-element.22.cos_ref, ...), custom_call_target="tpu_custom_call" | custom-call | tf_op jit(solution)/shard_map/prep/pallas_call | solution.py:224
  7.0 0.0 copy-start
  7.0 10.5 %all_to_all.16 = s32[16,1,2]{2,1,0:T(1,128)} all-to-all(s32[16,1,2]{2,1,0:T(1,128)} %bitcast.9), channel_id=1, replica_groups=mesh['groups'=2,'ctx'=16] {'ctx'}, dimensions={0} | all-to-all | bytes 256 | tf_op jit(solution)/shard_map/all_to_all | solution.py:240
  17.5 65.7 %gather.1 = bf16[16,2,128,256]{3,2,1,0:T(8,128)(2,1)} custom-call(s32[16,2]{1,0:T(8,128)} %bitcast.8, bf16[2,8,128,256]{3,2,1,0:T(8,128)(2,1)} %get-tuple-element.14.own_ref.kv_ref), custom_call_target="tpu_custom_call" | custom-call | tf_op jit(solution)/shard_map/gather/pallas_call | solution.py:242
  83.3 6.1 %all-to-all-start.1 = ((bf16[16,2,128,256]{3,2,1,0:T(8,128)(2,1)}), bf16[16,2,128,256]{3,2,1,0:T(8,128)(2,1)S(1)}, u32[]{:S(2)}, u32[]{:S(2)}) async-start(bf16[16,2,128,256]{3,2,1,0:T(8,128)(2,1)} %gather.1), calls=%async_computation.1 | async-start | bytes 4194304 | tf_op jit(solution)/shard_map/all_to_all | solution.py:250
  89.4 0.0 copy-done
  89.4 3.4 %collective-permute-start.1 = (bf16[2,8,128,256]{3,2,1,0:T(8,128)(2,1)S(1)}, bf16[2,8,128,256]{3,2,1,0:T(8,128)(2,1)}, u32[]{:S(2)}, u32[]{:S(2)}) collective-permute-start(bf16[2,8,128,256]{3,2,1,0:T(8,128)(2,1)S(1)} %copy-done), channel_id=1, source_target_pairs={{0,1},{1,2},{2,3},{3,4},{4,5},{5,6},{6,7},{7,8},{8,9},{9,10},{10,1... | collective-permute-start | bytes 3145736 | tf_op jit(solution)/shard_map/ppermute | solution.py:34
  92.7 3.1 %collective-permute-start = (bf16[1,8,128,256]{3,2,1,0:T(8,128)(2,1)}, bf16[1,8,128,256]{3,2,1,0:T(8,128)(2,1)}, u32[]{:S(2)}, u32[]{:S(2)}) collective-permute-start(bf16[1,8,128,256]{3,2,1,0:T(8,128)(2,1)} %get-tuple-element.13), channel_id=1, source_target_pairs={{0,2},{1,3},{2,4},{3,5},{4,6},{5,7},{6,8},{7,9},{8,10},{9,11},{10,... | collective-permute-start | bytes 1572872 | tf_op jit(solution)/shard_map/ppermute | solution.py:34
  95.8 63.4 %collective-permute-done.far_ref = bf16[1,8,128,256]{3,2,1,0:T(8,128)(2,1)} collective-permute-done((bf16[1,8,128,256]{3,2,1,0:T(8,128)(2,1)}, bf16[1,8,128,256]{3,2,1,0:T(8,128)(2,1)}, u32[]{:S(2)}, u32[]{:S(2)}) %collective-permute-start) | collective-permute-done | bytes 524320 | tf_op jit(solution)/shard_map/ppermute | solution.py:34
  159.3 0.0 collective-permute-done.1.near_ref
  159.3 0.0 copy-done.1
  159.3 0.0 copy-done.2
  159.3 0.0 copy-start.3
  159.3 2.2 %copy-done.3 = bf16[256,8192]{1,0:T(8,128)(2,1)S(1)} copy-done((bf16[256,8192]{1,0:T(8,128)(2,1)S(1)}, bf16[256,8192]{1,0:T(8,128)(2,1)}, u32[]{:S(2)}) %copy-start.3) | copy-done | bytes 4194328
  161.5 0.0 copy-start.4
  161.5 16.9 %band.1 = (bf16[2,8,1024,128]{3,2,1,0:T(8,128)(2,1)S(1)}, bf16[2,8,1024,128]{3,2,1,0:T(8,128)(2,1)S(1)}, f32[2,8,128,128]{3,2,1,0:T(8,128)S(1)}) custom-call(s32[1]{0:T(128)} %bitcast.me_ref, bf16[256,8192]{1,0:T(8,128)(2,1)S(1)} %copy-done.3, f32[256,128]{1,0:T(8,128)S(1)} %copy-done.1, f32[256,128]{1,0:T(8,128)S(1)} %copy-done.2, ...), custom_call_target="tpu_custom_call" | custom-call | flops 17179869184 | bytes 16777216 | tf_op jit(solution)/shard_map/band/pallas_call | solution.py:255
  178.4 0.0 copy-start.5
  178.5 2.0 copy-done.5
  180.5 0.0 copy-start.7
  180.5 2.0 copy-done.7
  182.4 0.0 copy-start.9
  182.4 1.0 copy-done.9
  183.4 0.0 all-to-all-done.1
  183.4 0.0 copy-done.4
  183.4 0.0 copy-start.6
  183.4 2.2 %copy-done.6 = bf16[2,8,1024,128]{3,2,1,0:T(8,128)(2,1)S(1)} copy-done((bf16[2,8,1024,128]{3,2,1,0:T(8,128)(2,1)S(1)}, bf16[2,8,1024,128]{3,2,1,0:T(8,128)(2,1)}, u32[]{:S(2)}) %copy-start.6) | copy-done | bytes 4194328
  185.6 0.0 copy-start.8
  185.6 2.2 %copy-done.8 = bf16[2,8,1024,128]{3,2,1,0:T(8,128)(2,1)S(1)} copy-done((bf16[2,8,1024,128]{3,2,1,0:T(8,128)(2,1)S(1)}, bf16[2,8,1024,128]{3,2,1,0:T(8,128)(2,1)}, u32[]{:S(2)}) %copy-start.8) | copy-done | bytes 4194328
  187.8 0.0 copy-start.10
  187.8 1.2 copy-done.10
  189.0 19.3 %picks.1 = bf16[256,8192]{1,0:T(8,128)(2,1)} custom-call(s32[16,2]{1,0:T(8,128)S(1)} %copy-done.4, bf16[2,8,1024,128]{3,2,1,0:T(8,128)(2,1)S(1)} %copy-done.6, bf16[32,128,256]{2,1,0:T(8,128)(2,1)S(1)} %bitcast.6, bf16[32,128,256]{2,1,0:T(8,128)(2,1)S(1)} %bitcast.7, bf16[2,8,1024,128]{3,2,1,0:T(8,128)(2,1)S(1)} %copy-done.8, f32[2,8,128,128]{3,2,1,0:T(8,128)S(1)} %copy-done.10), custom_call_target="tpu_custom_call" | custom-call | flops 8589934592 | bytes 16777216 | tf_op jit(solution)/shard_map/picks/pallas_call | solution.py:290
  (1 shorter events, 0.0 us)
Async XLA Ops:
  3.4 155.9 %copy-start.1 = (f32[256,128]{1,0:T(8,128)S(1)}, f32[256,128]{1,0:T(8,128)}, u32[]{:S(2)}) copy-start(f32[256,128]{1,0:T(8,128)} %get-tuple-element.22.cos_ref) | copy-start | bytes 393220
  3.4 155.9 %copy-start.2 = (f32[256,128]{1,0:T(8,128)S(1)}, f32[256,128]{1,0:T(8,128)}, u32[]{:S(2)}) copy-start(f32[256,128]{1,0:T(8,128)} %get-tuple-element.23.sin_ref) | copy-start | bytes 393220
  7.0 82.4 %copy-start = (bf16[2,8,128,256]{3,2,1,0:T(8,128)(2,1)S(1)}, bf16[2,8,128,256]{3,2,1,0:T(8,128)(2,1)}, u32[]{:S(2)}) copy-start(bf16[2,8,128,256]{3,2,1,0:T(8,128)(2,1)} %get-tuple-element.14.own_ref.kv_ref) | copy-start | bytes 3145732
  83.3 100.2 %all-to-all-start.1 = ((bf16[16,2,128,256]{3,2,1,0:T(8,128)(2,1)}), bf16[16,2,128,256]{3,2,1,0:T(8,128)(2,1)S(1)}, u32[]{:S(2)}, u32[]{:S(2)}) async-start(bf16[16,2,128,256]{3,2,1,0:T(8,128)(2,1)} %gather.1), calls=%async_computation.1 | async-start | bytes 4194304 | tf_op jit(solution)/shard_map/all_to_all | solution.py:250
  89.4 69.9 %collective-permute-start.1 = (bf16[2,8,128,256]{3,2,1,0:T(8,128)(2,1)S(1)}, bf16[2,8,128,256]{3,2,1,0:T(8,128)(2,1)}, u32[]{:S(2)}, u32[]{:S(2)}) collective-permute-start(bf16[2,8,128,256]{3,2,1,0:T(8,128)(2,1)S(1)} %copy-done), channel_id=1, source_target_pairs={{0,1},{1,2},{2,3},{3,4},{4,5},{5,6},{6,7},{7,8},{8,9},{9,10},{10,1... | collective-permute-start | bytes 3145736 | tf_op jit(solution)/shard_map/ppermute | solution.py:34
  92.7 66.6 %collective-permute-start = (bf16[1,8,128,256]{3,2,1,0:T(8,128)(2,1)}, bf16[1,8,128,256]{3,2,1,0:T(8,128)(2,1)}, u32[]{:S(2)}, u32[]{:S(2)}) collective-permute-start(bf16[1,8,128,256]{3,2,1,0:T(8,128)(2,1)} %get-tuple-element.13), channel_id=1, source_target_pairs={{0,2},{1,3},{2,4},{3,5},{4,6},{5,7},{6,8},{7,9},{8,10},{9,11},{10,... | collective-permute-start | bytes 1572872 | tf_op jit(solution)/shard_map/ppermute | solution.py:34
  159.3 2.2 %copy-start.3 = (bf16[256,8192]{1,0:T(8,128)(2,1)S(1)}, bf16[256,8192]{1,0:T(8,128)(2,1)}, u32[]{:S(2)}) copy-start(bf16[256,8192]{1,0:T(8,128)(2,1)} %q_ref.1) | copy-start | bytes 12582916
  161.5 21.9 %copy-start.4 = (s32[16,2]{1,0:T(8,128)S(1)}, s32[16,2]{1,0:T(8,128)}, u32[]{:S(2)}) copy-start(s32[16,2]{1,0:T(8,128)} %get-tuple-element.12.slot_ref) | copy-start | bytes 388
  178.4 2.0 copy-start.5
  180.5 2.0 copy-start.7
  182.4 1.0 copy-start.9
  183.4 2.2 %copy-start.6 = (bf16[2,8,1024,128]{3,2,1,0:T(8,128)(2,1)S(1)}, bf16[2,8,1024,128]{3,2,1,0:T(8,128)(2,1)}, u32[]{:S(2)}) copy-start(bf16[2,8,1024,128]{3,2,1,0:T(8,128)(2,1)} %copy-done.5) | copy-start | bytes 12582916
  185.6 2.2 %copy-start.8 = (bf16[2,8,1024,128]{3,2,1,0:T(8,128)(2,1)S(1)}, bf16[2,8,1024,128]{3,2,1,0:T(8,128)(2,1)}, u32[]{:S(2)}) copy-start(bf16[2,8,1024,128]{3,2,1,0:T(8,128)(2,1)} %copy-done.7) | copy-start | bytes 12582916
  187.8 1.2 copy-start.10
where the time goes:
time: 209 us; the launch traced here: 208 us
  Pallas kernels  105 us (50%)
  waiting for transfers between devices  63.5 us (30%)
  local copies, waits for them, and re-layouts  14.1 us (7%)
  starting transfers between devices  12.6 us (6%)
  blocking collectives  10.5 us (5%)
    pallas_call x1, Pallas kernels, shards(): pl.pallas_call(gather_kernel, out_shape=jax.ShapeDtypeStruct((window, lim...  65.7 us
    ppermute x2, waiting for transfers between devices, from_behind(): return lax.ppermute(block, axis, route)  63.4 us
    pallas_call x1, Pallas kernels, shards(): pl.pallas_call(picks_kernel, out_shape=jax.ShapeDtypeStruct((tokens, QUER...  19.3 us
    pallas_call x1, Pallas kernels, shards(): pl.pallas_call(band_kernel, out_shape=(jax.ShapeDtypeStruct((BLOCKS, KEY_...  16.9 us
    unnamed x23, local copies, waits for them, and re-layouts  14.1 us
    all_to_all x1, blocking collectives, shards(): lax.all_to_all(table, 'ctx', split_axis=0, concat_axis=0, tiled=True)  10.5 us
    ppermute x2, starting transfers between devices, from_behind(): return lax.ppermute(block, axis, route)  6.46 us
    all_to_all x1, starting transfers between devices, shards(): lax.all_to_all(answer, 'ctx', split_axis=0, concat_axis=0, tiled=True)  6.11 us
  transfers between devices with their start and end apart: 3, of which 1 were waited for; matrix products, arithmetic and copies ran while one was open for 0% of the time, Pallas kernels for 8%

commit v1 on v0

v1 whole, which is shorter than its diff:
```python
import functools

import jax
import jax.numpy as jnp
from jax import lax
from jax.experimental import pallas as pl
from jax.experimental.pallas import tpu as pltpu
from jax.sharding import PartitionSpec as P

QUERY_HEADS = 64
KEY_VALUE_HEADS = 8
HEAD_SIZE = 128
BLOCK_TOKENS = 128
LOCAL_BAND_SIZE = 4
PICKED_BLOCKS = 2
GROUP = QUERY_HEADS // KEY_VALUE_HEADS
ROWS = GROUP * BLOCK_TOKENS
PAIR = 2 * HEAD_SIZE
BLOCKS = 2

rope_base = 500000.0
masked_score = -1e30
score_factor = HEAD_SIZE ** (-0.5) * 1.4426950408889634

BAND_ROWS = 256
PICK_ROWS = 512
PICK_UNROLL = 4
PICK_AHEAD = 2

SMEM = pltpu.MemorySpace.SMEM


def from_behind(block, axis, distance):
    devices = range(lax.axis_size(axis))
    route = [(i - distance, i) for i in devices if i - distance in devices]
    return lax.ppermute(block, axis, route)


def rotary_tables(pos):
    half = HEAD_SIZE // 2
    freq = rope_base ** (-(jnp.arange(half, dtype=jnp.float32) * 2.0) / HEAD_SIZE)
    angle = pos.astype(jnp.float32)[:, None] * freq[None, :]
    cosine = jnp.cos(angle)
    sine = jnp.sin(angle)
    return jnp.concatenate([cosine, cosine], -1), jnp.concatenate([-sine, sine], -1)


def rotate(x, cosine, sine):
    wide = x.astype(jnp.float32)
    swapped = pltpu.roll(wide, HEAD_SIZE // 2, 1)
    return (wide * cosine + swapped * sine).astype(jnp.bfloat16)


def prep_kernel(limit, picks_ref, k_ref, v_ref, cos_ref, sin_ref, kv_ref, last_ref, table_ref, slot_ref, count_ref):
    shards = table_ref.shape[0]

    @pl.loop(0, shards)
    def _(i):
        count_ref[i] = 0
        for r in range(limit):
            table_ref[i, r] = -1

    @pl.loop(0, BLOCKS * KEY_VALUE_HEADS)
    def _(i):
        b = i // KEY_VALUE_HEADS
        h = i % KEY_VALUE_HEADS
        for p in range(PICKED_BLOCKS):
            pick = picks_ref[b, h, p]
            slot_ref[i, p] = -1

            @pl.when(pick >= 0)
            def _():
                owner = pick // BLOCKS
                rank = jnp.minimum(count_ref[owner], limit - 1)
                count_ref[owner] = rank + 1
                table_ref[owner, rank] = pick % BLOCKS * KEY_VALUE_HEADS + h
                slot_ref[i, p] = owner * limit + rank

    for b in range(BLOCKS):
        rows = slice(b * BLOCK_TOKENS, (b + 1) * BLOCK_TOKENS)
        cosine = cos_ref[rows, :]
        sine = sin_ref[rows, :]
        for h in range(KEY_VALUE_HEADS):
            cols = slice(h * HEAD_SIZE, (h + 1) * HEAD_SIZE)
            rotated = rotate(k_ref[rows, cols], cosine, sine)
            value = v_ref[rows, cols]
            kv_ref[b, h, :, :HEAD_SIZE] = rotated
            kv_ref[b, h, :, HEAD_SIZE:] = value
            if b == BLOCKS - 1:
                last_ref[0, h, :, :HEAD_SIZE] = rotated
                last_ref[0, h, :, HEAD_SIZE:] = value


def gather_kernel(wanted_ref, kv_ref, out_ref, sems):
    shards, limit = wanted_ref.shape

    def copy(i, r):
        entry = jnp.maximum(wanted_ref[i, r], 0)
        return pltpu.make_async_copy(
            kv_ref.at[entry // KEY_VALUE_HEADS, entry % KEY_VALUE_HEADS],
            out_ref.at[i, r],
            sems.at[i, r],
        )

    @pl.loop(0, shards)
    def _(i):
        for r in range(limit):
            copy(i, r).start()

    @pl.loop(0, shards)
    def _(i):
        for r in range(limit):
            copy(i, r).wait()


def scores_of(query, key):
    return lax.dot_general(query, key, (((1,), (1,)), ((), ())), preferred_element_type=jnp.float32)


def summed(weight, value):
    both = jnp.concatenate([value, jnp.ones_like(value)], 1)
    out = jnp.dot(weight, both, preferred_element_type=jnp.float32)
    return out[:, :HEAD_SIZE], out[:, HEAD_SIZE:]


def band_kernel(me_ref, q_ref, cos_ref, sin_ref, far_ref, near_ref, own_ref, qr_ref, acc_ref, lse_ref):
    me = me_ref[0]
    row = lax.broadcasted_iota(jnp.int32, (BLOCK_TOKENS, BLOCK_TOKENS), 0)
    col = lax.broadcasted_iota(jnp.int32, (BLOCK_TOKENS, BLOCK_TOKENS), 1)
    causal = jnp.concatenate([col <= row] * (BAND_ROWS // BLOCK_TOKENS), 0)
    edge = (LOCAL_BAND_SIZE - 1) * BLOCK_TOKENS

    def attend(start, h):
        cols = pl.ds(pl.multiple_of(h * ROWS, ROWS), ROWS)
        pieces = [far_ref[0, h], near_ref[0, h], near_ref[1, h], own_ref[0, h], own_ref[1, h]]
        for b in range(BLOCKS):
            rows = slice(b * BLOCK_TOKENS, (b + 1) * BLOCK_TOKENS)
            query = q_ref[rows, cols]
            cosine = cos_ref[rows, :]
            sine = sin_ref[rows, :]
            window = jnp.concatenate(pieces[b : b + LOCAL_BAND_SIZE], 0)
            key = window[:, :HEAD_SIZE]
            value = window[:, HEAD_SIZE:]
            for first in range(0, ROWS, BAND_ROWS):
                part = slice(first, first + BAND_ROWS)
                rotated = jnp.concatenate(
                    [
                        rotate(query[:, at : at + HEAD_SIZE], cosine, sine)
                        for at in range(first, first + BAND_ROWS, HEAD_SIZE)
                    ],
                    0,
                )
                qr_ref[b, h, part, :] = rotated
                score = scores_of(rotated, key)
                before = score[:, :edge]
                if start:
                    oldest = (me * BLOCKS + b - (LOCAL_BAND_SIZE - 1)) * BLOCK_TOKENS
                    index = oldest + lax.broadcasted_iota(jnp.int32, before.shape, 1)
                    before = jnp.where(index >= 0, before, masked_score)
                score = jnp.concatenate([before, jnp.where(causal, score[:, edge:], masked_score)], 1)
                top = jnp.max(score, -1, keepdims=True) * score_factor
                weight = jnp.exp2(score * score_factor - top)
                out, total = summed(weight.astype(jnp.bfloat16), value)
                acc_ref[b, h, part, :] = (out / total).astype(acc_ref.dtype)
                lse_ref[b, h, part, :] = jnp.log2(total) + top

    early = me * BLOCKS < LOCAL_BAND_SIZE - 1

    @pl.when(early)
    def _():
        pl.loop(0, KEY_VALUE_HEADS)(functools.partial(attend, True))

    @pl.when(jnp.logical_not(early))
    def _():
        pl.loop(0, KEY_VALUE_HEADS)(functools.partial(attend, False))


def picks_kernel(
    slot_ref, q_hbm, landed_hbm, acc_hbm, lse_hbm, out_ref, q_ref, piece_ref, acc_ref, lse_ref, stage_ref, ins, sems
):
    count = BLOCKS * KEY_VALUE_HEADS
    rounds = count // PICK_UNROLL

    def send(i):
        b = i // KEY_VALUE_HEADS
        h = i % KEY_VALUE_HEADS
        return pltpu.make_async_copy(
            stage_ref.at[i],
            out_ref.at[
                pl.ds(pl.multiple_of(b * BLOCK_TOKENS, BLOCK_TOKENS), BLOCK_TOKENS),
                pl.ds(pl.multiple_of(h * ROWS, ROWS), ROWS),
            ],
            sems.at[i],
        )

    def loads(i):
        b = i // KEY_VALUE_HEADS
        h = i % KEY_VALUE_HEADS
        pairs = [
            (landed_hbm.at[jnp.maximum(slot_ref[i, p], 0)], piece_ref.at[i, p]) for p in range(PICKED_BLOCKS)
        ] + [
            (q_hbm.at[b, h], q_ref.at[b, h]),
            (lse_hbm.at[b, h], lse_ref.at[b, h]),
            (acc_hbm.at[b, h], acc_ref.at[b, h]),
        ]
        return [pltpu.make_async_copy(src, dst, ins.at[i, n]) for n, (src, dst) in enumerate(pairs)]

    def start_round(j):
        for u in range(PICK_UNROLL):
            for copy in loads(j * PICK_UNROLL + u):
                copy.start()

    for j in range(min(PICK_AHEAD, rounds)):
        start_round(j)

    @pl.loop(0, rounds)
    def _(j):
        @pl.when(j + PICK_AHEAD < rounds)
        def _():
            start_round(j + PICK_AHEAD)

        for u in range(PICK_UNROLL):
            for copy in loads(j * PICK_UNROLL + u):
                copy.wait()

        for u in range(PICK_UNROLL):
            i = j * PICK_UNROLL + u
            b = i // KEY_VALUE_HEADS
            h = i % KEY_VALUE_HEADS
            bias = jnp.where(slot_ref[i, 0] >= 0, 0.0, masked_score)
            window = piece_ref[i].reshape(PICKED_BLOCKS * BLOCK_TOKENS, PAIR)
            key = window[:, :HEAD_SIZE]
            value = window[:, HEAD_SIZE:]
            for first in range(0, ROWS, PICK_ROWS):
                part = slice(first, first + PICK_ROWS)
                score = scores_of(q_ref[b, h, part, :], key)
                old = lse_ref[b, h, part, :]
                best = jnp.broadcast_to(jnp.max(score, -1, keepdims=True) * score_factor, old.shape) + bias
                top = jnp.maximum(best, old)
                shift = top - bias
                weight = jnp.exp2(score * score_factor - jnp.concatenate([shift] * PICKED_BLOCKS, 1))
                fade = jnp.exp2(old - top)
                out, total = summed(weight.astype(jnp.bfloat16), value)
                out = out + acc_ref[b, h, part, :].astype(jnp.float32) * fade
                result = (out / (total + fade)).astype(stage_ref.dtype)
                for g in range(PICK_ROWS // BLOCK_TOKENS):
                    at = slice(g * BLOCK_TOKENS, (g + 1) * BLOCK_TOKENS)
                    stage_ref[i, :, first + g * HEAD_SIZE : first + (g + 1) * HEAD_SIZE] = result[at]
            send(i).start()

    for i in range(count):
        send(i).wait()


def shards(queries, keys, values, positions, picks):
    tokens = queries.shape[0]
    window = lax.axis_size("ctx")
    limit = max(1, BLOCKS * KEY_VALUE_HEADS * PICKED_BLOCKS // window)
    me = lax.axis_index("ctx").astype(jnp.int32).reshape(1)
    cosine, sine = rotary_tables(positions)
    bf16 = jnp.bfloat16
    vmem = pl.BlockSpec(memory_space=pltpu.MemorySpace.VMEM)
    smem = pl.BlockSpec(memory_space=SMEM)
    hbm = pl.BlockSpec(memory_space=pl.ANY)

    kv, last, table, slot = pl.pallas_call(
        functools.partial(prep_kernel, limit),
        out_shape=(
            jax.ShapeDtypeStruct((BLOCKS, KEY_VALUE_HEADS, BLOCK_TOKENS, PAIR), bf16),
            jax.ShapeDtypeStruct((1, KEY_VALUE_HEADS, BLOCK_TOKENS, PAIR), bf16),
            jax.ShapeDtypeStruct((window, limit), jnp.int32),
            jax.ShapeDtypeStruct((BLOCKS * KEY_VALUE_HEADS, PICKED_BLOCKS), jnp.int32),
        ),
        in_specs=[smem, vmem, vmem, vmem, vmem],
        out_specs=(vmem, vmem, smem, smem),
        scratch_shapes=[pltpu.SMEM((window,), jnp.int32)],
        name="prep",
    )(picks, keys, values, cosine, sine)

    near = from_behind(kv, "ctx", 1)
    far = from_behind(last, "ctx", 2)
    wanted = lax.all_to_all(table, "ctx", split_axis=0, concat_axis=0, tiled=True)

    answer = pl.pallas_call(
        gather_kernel,
        out_shape=jax.ShapeDtypeStruct((window, limit, BLOCK_TOKENS, PAIR), bf16),
        in_specs=[smem, vmem],
        out_specs=hbm,
        scratch_shapes=[pltpu.SemaphoreType.DMA((window, limit))],
        cost_estimate=pl.CostEstimate(flops=0, bytes_accessed=60 << 20, transcendentals=0),
        name="gather",
    )(wanted, kv)
    landed = lax.all_to_all(answer, "ctx", split_axis=0, concat_axis=0, tiled=True)
    landed = landed.reshape(window * limit, BLOCK_TOKENS, PAIR)

    band_flops = 4 * BLOCKS * QUERY_HEADS * BLOCK_TOKENS * LOCAL_BAND_SIZE * BLOCK_TOKENS * HEAD_SIZE
    full = (BLOCKS, KEY_VALUE_HEADS, ROWS, HEAD_SIZE)
    rotated, acc, lse = pl.pallas_call(
        band_kernel,
        out_shape=(
            jax.ShapeDtypeStruct(full, bf16),
            jax.ShapeDtypeStruct(full, bf16),
            jax.ShapeDtypeStruct(full, jnp.float32),
        ),
        in_specs=[smem] + [vmem] * 6,
        out_specs=(vmem,) * 3,
        cost_estimate=pl.CostEstimate(flops=100 * band_flops, bytes_accessed=16 << 20, transcendentals=1 << 23),
        compiler_params=pltpu.CompilerParams(vmem_limit_bytes=30 << 20),
        name="band",
    )(me, queries, cosine, sine, far, near, kv)

    return pl.pallas_call(
        picks_kernel,
        out_shape=jax.ShapeDtypeStruct((tokens, QUERY_HEADS * HEAD_SIZE), bf16),
        in_specs=[smem] + [hbm] * 4,
        out_specs=hbm,
        scratch_shapes=[
            pltpu.VMEM(full, bf16),
            pltpu.VMEM((BLOCKS * KEY_VALUE_HEADS, PICKED_BLOCKS, BLOCK_TOKENS, PAIR), bf16),
            pltpu.VMEM(full, bf16),
            pltpu.VMEM(full, jnp.float32),
            pltpu.VMEM((BLOCKS * KEY_VALUE_HEADS, BLOCK_TOKENS, ROWS), bf16),
            pltpu.SemaphoreType.DMA((BLOCKS * KEY_VALUE_HEADS, PICKED_BLOCKS + 3)),
            pltpu.SemaphoreType.DMA((BLOCKS * KEY_VALUE_HEADS,)),
        ],
        cost_estimate=pl.CostEstimate(flops=2 * band_flops, bytes_accessed=16 << 20, transcendentals=1 << 22),
        compiler_params=pltpu.CompilerParams(vmem_limit_bytes=58 << 20),
        name="picks",
    )(slot, rotated, landed, acc, lse)


def solution(mesh):
    return jax.shard_map(
        shards,
        mesh=mesh,
        in_specs=(
            P(("groups", "ctx"), None),
            P(("groups", "ctx"), None),
            P(("groups", "ctx"), None),
            P(("groups", "ctx")),
            P(("groups", "ctx"), None, None),
        ),
        out_specs=P(("groups", "ctx"), None),
        check_vma=False,
    )
```

time: 209 us -> 106 us (0.51)
  the two profiles are of different devices: /device:TPU:17 before, /device:TPU:15 now
where the time goes in v1:
time: 106 us
  waiting for transfers between devices  38.6 us (36%)
  Pallas kernels  35.3 us (33%)
  starting transfers between devices  18.5 us (17%)
  local copies, waits for them, and re-layouts  11.3 us (11%)
  other arithmetic  2.07 us (2%)
    all_to_all x1, waiting for transfers between devices, shards(): lax.all_to_all(answer, 'ctx', split_axis=0, concat_axis=0, tiled=True)  22.8 us
    all_to_all x1, waiting for transfers between devices, shards(): lax.all_to_all(table, 'ctx', split_axis=0, concat_axis=0, tiled=True)  15.8 us
    pallas_call x1, Pallas kernels, shards(): pl.pallas_call(band_kernel, out_shape=(jax.ShapeDtypeStruct(full, bf16),...  15.3 us
    pallas_call x1, Pallas kernels, shards(): pl.pallas_call(picks_kernel, out_shape=jax.ShapeDtypeStruct((tokens, QUER...  13.6 us
    unnamed x17, local copies, waits for them, and re-layouts  11.3 us
    ppermute x2, starting transfers between devices, from_behind(): return lax.ppermute(block, axis, route)  6.99 us
    all_to_all x1, starting transfers between devices, shards(): lax.all_to_all(answer, 'ctx', split_axis=0, concat_axis=0, tiled=True)  6.51 us
    all_to_all x1, starting transfers between devices, shards(): lax.all_to_all(table, 'ctx', split_axis=0, concat_axis=0, tiled=True)  4.99 us
  transfers between devices with their start and end apart: 4, of which 2 were waited for; matrix products, arithmetic and copies ran while one was open for 0% of the time, Pallas kernels for 17%

profile of v1, /device:TPU:15, one launch (start us, length us, event | category | flops | bytes accessed | tf_op | source)
XLA Modules:
  0.0 105.9 jit_solution(13538219401489865050)
XLA Ops:
  0.0 0.7 convert_element_type.3
  0.7 1.4 %copy.9.picks_ref = s32[2,8,2]{2,1,0:T(8,128)} copy(s32[2,8,2]{1,2,0:T(2,128)} %param.9) | data formatting | bytes 256 | tf_op args[4]
  2.1 0.5 fusion
  2.6 0.8 pad_maximum_fusion
  3.4 0.0 copy-start.1
  3.4 0.0 copy-start.2
  3.4 3.6 %prep.1 = (bf16[2,8,128,256]{3,2,1,0:T(8,128)(2,1)}, bf16[1,8,128,256]{3,2,1,0:T(8,128)(2,1)}, s32[16,2]{1,0:T(8,128)}, s32[16,2]{1,0:T(8,128)}) custom-call(s32[2,8,2]{2,1,0:T(8,128)} %copy.9.picks_ref, bf16[256,1024]{1,0:T(8,128)(2,1)} %k_ref.1, bf16[256,1024]{1,0:T(8,128)(2,1)} %v_ref.1, f32[256,128]{1,0:T(8,128)} %get-tuple-element.22.cos_ref, ...), custom_call_target="tpu_custom_call" | custom-call | tf_op jit(solution)/shard_map/prep/pallas_call | solution.py:266
  7.0 0.0 copy-start
  7.0 3.9 %collective-permute-start.1 = (bf16[2,8,128,256]{3,2,1,0:T(8,128)(2,1)}, bf16[2,8,128,256]{3,2,1,0:T(8,128)(2,1)S(1)}, u32[]{:S(2)}, u32[]{:S(2)}) collective-permute-start(bf16[2,8,128,256]{3,2,1,0:T(8,128)(2,1)} %get-tuple-element.14.own_ref.kv_ref), channel_id=1, source_target_pairs={{0,1},{1,2},{2,3},{3,4},{4,5},{5,6},{6,7},{7,8},{8,9},{9,10},{10,1... | collective-permute-start | bytes 3145736 | tf_op jit(solution)/shard_map/ppermute | solution.py:36
  10.9 3.1 %collective-permute-start = (bf16[1,8,128,256]{3,2,1,0:T(8,128)(2,1)}, bf16[1,8,128,256]{3,2,1,0:T(8,128)(2,1)S(1)}, u32[]{:S(2)}, u32[]{:S(2)}) collective-permute-start(bf16[1,8,128,256]{3,2,1,0:T(8,128)(2,1)} %get-tuple-element.13), channel_id=1, source_target_pairs={{0,2},{1,3},{2,4},{3,5},{4,6},{5,7},{6,8},{7,9},{8,10},{9,11},{10,... | collective-permute-start | bytes 1572872 | tf_op jit(solution)/shard_map/ppermute | solution.py:36
  14.0 5.0 %all-to-all-start = ((s32[16,1,2]{2,1,0:T(1,128)}), s32[16,1,2]{2,1,0:T(1,128)S(1)}, u32[]{:S(2)}, u32[]{:S(2)}) async-start(s32[16,1,2]{2,1,0:T(1,128)} %bitcast.7), calls=%async_computation | async-start | bytes 16384 | tf_op jit(solution)/shard_map/all_to_all | solution.py:282
  19.0 15.8 %all-to-all-done = s32[16,1,2]{2,1,0:T(1,128)S(1)} async-done(((s32[16,1,2]{2,1,0:T(1,128)}), s32[16,1,2]{2,1,0:T(1,128)S(1)}, u32[]{:S(2)}, u32[]{:S(2)}) %all-to-all-start) | async-done | bytes 160 | tf_op jit(solution)/shard_map/all_to_all | solution.py:282
  34.8 0.0 copy-start.7
  34.8 0.6 copy-done.7
  35.4 2.8 %gather.1 = bf16[16,2,128,256]{3,2,1,0:T(8,128)(2,1)} custom-call(s32[16,2]{1,0:T(8,128)} %bitcast.6, bf16[2,8,128,256]{3,2,1,0:T(8,128)(2,1)} %get-tuple-element.14.own_ref.kv_ref), custom_call_target="tpu_custom_call" | custom-call | bytes 62914560 | tf_op jit(solution)/shard_map/gather/pallas_call | solution.py:284
  38.3 6.5 %all-to-all-start.1 = ((bf16[16,2,128,256]{3,2,1,0:T(8,128)(2,1)}), bf16[16,2,128,256]{3,2,1,0:T(8,128)(2,1)}, u32[]{:S(2)}, u32[]{:S(2)}) async-start(bf16[16,2,128,256]{3,2,1,0:T(8,128)(2,1)} %gather.1), calls=%async_computation.1 | async-start | bytes 4194304 | tf_op jit(solution)/shard_map/all_to_all | solution.py:293
  44.8 0.0 collective-permute-done.far_ref
  44.8 0.0 collective-permute-done.1.near_ref
  44.8 0.0 copy-done.1
  44.8 0.0 copy-done.2
  44.8 0.0 copy-done
  44.8 0.0 copy-start.3
  44.8 2.2 %copy-done.3 = bf16[256,8192]{1,0:T(8,128)(2,1)S(1)} copy-done((bf16[256,8192]{1,0:T(8,128)(2,1)S(1)}, bf16[256,8192]{1,0:T(8,128)(2,1)}, u32[]{:S(2)}) %copy-start.3) | copy-done | bytes 4194328
  47.0 15.3 %band.1 = (bf16[2,8,1024,128]{3,2,1,0:T(8,128)(2,1)S(1)}, bf16[2,8,1024,128]{3,2,1,0:T(8,128)(2,1)S(1)}, f32[2,8,1024,128]{3,2,1,0:T(8,128)S(1)}) custom-call(s32[1]{0:T(128)} %bitcast.me_ref, bf16[256,8192]{1,0:T(8,128)(2,1)S(1)} %copy-done.3, f32[256,128]{1,0:T(8,128)S(1)} %copy-done.1, f32[256,128]{1,0:T(8,128)S(1)} %copy-done.2, ...), custom_call_target="tpu_custom_call" | custom-call | flops 429496729600 | bytes 16777216 | tf_op jit(solution)/shard_map/band/pallas_call | solution.py:298
  62.3 0.0 copy-start.4
  62.3 3.2 %copy-done.4 = f32[2,8,1024,128]{3,2,1,0:T(8,128)} copy-done((f32[2,8,1024,128]{3,2,1,0:T(8,128)}, f32[2,8,1024,128]{3,2,1,0:T(8,128)S(1)}, u32[]{:S(2)}) %copy-start.4) | copy-done | bytes 8388632
  65.6 0.0 copy-start.5
  65.6 2.0 %copy-done.5 = bf16[2,8,1024,128]{3,2,1,0:T(8,128)(2,1)} copy-done((bf16[2,8,1024,128]{3,2,1,0:T(8,128)(2,1)}, bf16[2,8,1024,128]{3,2,1,0:T(8,128)(2,1)S(1)}, u32[]{:S(2)}) %copy-start.5) | copy-done | bytes 4194328
  67.5 0.0 copy-start.6
  67.5 1.9 %copy-done.6 = bf16[2,8,1024,128]{3,2,1,0:T(8,128)(2,1)} copy-done((bf16[2,8,1024,128]{3,2,1,0:T(8,128)(2,1)}, bf16[2,8,1024,128]{3,2,1,0:T(8,128)(2,1)S(1)}, u32[]{:S(2)}) %copy-start.6) | copy-done | bytes 4194328
  69.5 22.8 %all-to-all-done.1 = bf16[16,2,128,256]{3,2,1,0:T(8,128)(2,1)} async-done(((bf16[16,2,128,256]{3,2,1,0:T(8,128)(2,1)}), bf16[16,2,128,256]{3,2,1,0:T(8,128)(2,1)}, u32[]{:S(2)}, u32[]{:S(2)}) %all-to-all-start.1) | async-done | bytes 2097184 | tf_op jit(solution)/shard_map/all_to_all | solution.py:293
  92.3 13.6 %picks.1 = bf16[256,8192]{1,0:T(8,128)(2,1)} custom-call(s32[16,2]{1,0:T(8,128)} %get-tuple-element.12.slot_ref, bf16[2,8,1024,128]{3,2,1,0:T(8,128)(2,1)} %copy-done.5, bf16[32,128,256]{2,1,0:T(8,128)(2,1)} %bitcast.3.landed_hbm, bf16[2,8,1024,128]{3,2,1,0:T(8,128)(2,1)} %copy-done.6, f32[2,8,1024,128]{3,2,1,0:T(8,128)} %copy-done.4), custom_call_target="tpu_custom_call" | custom-call | flops 8589934592 | bytes 16777216 | tf_op jit(solution)/shard_map/picks/pallas_call | solution.py:312
  (1 shorter events, 0.0 us)
Async XLA Ops:
  3.4 41.3 %copy-start.1 = (f32[256,128]{1,0:T(8,128)S(1)}, f32[256,128]{1,0:T(8,128)}, u32[]{:S(2)}) copy-start(f32[256,128]{1,0:T(8,128)} %get-tuple-element.22.cos_ref) | copy-start | bytes 393220
  3.4 41.3 %copy-start.2 = (f32[256,128]{1,0:T(8,128)S(1)}, f32[256,128]{1,0:T(8,128)}, u32[]{:S(2)}) copy-start(f32[256,128]{1,0:T(8,128)} %get-tuple-element.23.sin_ref) | copy-start | bytes 393220
  7.0 37.8 %copy-start = (bf16[2,8,128,256]{3,2,1,0:T(8,128)(2,1)S(1)}, bf16[2,8,128,256]{3,2,1,0:T(8,128)(2,1)}, u32[]{:S(2)}) copy-start(bf16[2,8,128,256]{3,2,1,0:T(8,128)(2,1)} %get-tuple-element.14.own_ref.kv_ref) | copy-start | bytes 3145732
  7.0 37.8 %collective-permute-start.1 = (bf16[2,8,128,256]{3,2,1,0:T(8,128)(2,1)}, bf16[2,8,128,256]{3,2,1,0:T(8,128)(2,1)S(1)}, u32[]{:S(2)}, u32[]{:S(2)}) collective-permute-start(bf16[2,8,128,256]{3,2,1,0:T(8,128)(2,1)} %get-tuple-element.14.own_ref.kv_ref), channel_id=1, source_target_pairs={{0,1},{1,2},{2,3},{3,4},{4,5},{5,6},{6,7},{7,8},{8,9},{9,10},{10,1... | collective-permute-start | bytes 3145736 | tf_op jit(solution)/shard_map/ppermute | solution.py:36
  10.9 33.9 %collective-permute-start = (bf16[1,8,128,256]{3,2,1,0:T(8,128)(2,1)}, bf16[1,8,128,256]{3,2,1,0:T(8,128)(2,1)S(1)}, u32[]{:S(2)}, u32[]{:S(2)}) collective-permute-start(bf16[1,8,128,256]{3,2,1,0:T(8,128)(2,1)} %get-tuple-element.13), channel_id=1, source_target_pairs={{0,2},{1,3},{2,4},{3,5},{4,6},{5,7},{6,8},{7,9},{8,10},{9,11},{10,... | collective-permute-start | bytes 1572872 | tf_op jit(solution)/shard_map/ppermute | solution.py:36
  14.0 20.8 %all-to-all-start = ((s32[16,1,2]{2,1,0:T(1,128)}), s32[16,1,2]{2,1,0:T(1,128)S(1)}, u32[]{:S(2)}, u32[]{:S(2)}) async-start(s32[16,1,2]{2,1,0:T(1,128)} %bitcast.7), calls=%async_computation | async-start | bytes 16384 | tf_op jit(solution)/shard_map/all_to_all | solution.py:282
  34.8 0.6 copy-start.7
  38.3 54.0 %all-to-all-start.1 = ((bf16[16,2,128,256]{3,2,1,0:T(8,128)(2,1)}), bf16[16,2,128,256]{3,2,1,0:T(8,128)(2,1)}, u32[]{:S(2)}, u32[]{:S(2)}) async-start(bf16[16,2,128,256]{3,2,1,0:T(8,128)(2,1)} %gather.1), calls=%async_computation.1 | async-start | bytes 4194304 | tf_op jit(solution)/shard_map/all_to_all | solution.py:293
  44.8 2.2 %copy-start.3 = (bf16[256,8192]{1,0:T(8,128)(2,1)S(1)}, bf16[256,8192]{1,0:T(8,128)(2,1)}, u32[]{:S(2)}) copy-start(bf16[256,8192]{1,0:T(8,128)(2,1)} %q_ref.1) | copy-start | bytes 12582916
  62.3 3.2 %copy-start.4 = (f32[2,8,1024,128]{3,2,1,0:T(8,128)}, f32[2,8,1024,128]{3,2,1,0:T(8,128)S(1)}, u32[]{:S(2)}) copy-start(f32[2,8,1024,128]{3,2,1,0:T(8,128)S(1)} %get-tuple-element.18.lse_hbm) | copy-start | bytes 25165828
  65.6 2.0 %copy-start.5 = (bf16[2,8,1024,128]{3,2,1,0:T(8,128)(2,1)}, bf16[2,8,1024,128]{3,2,1,0:T(8,128)(2,1)S(1)}, u32[]{:S(2)}) copy-start(bf16[2,8,1024,128]{3,2,1,0:T(8,128)(2,1)S(1)} %get-tuple-element.15.q_hbm) | copy-start | bytes 12582916
  67.5 1.9 %copy-start.6 = (bf16[2,8,1024,128]{3,2,1,0:T(8,128)(2,1)}, bf16[2,8,1024,128]{3,2,1,0:T(8,128)(2,1)S(1)}, u32[]{:S(2)}) copy-start(bf16[2,8,1024,128]{3,2,1,0:T(8,128)(2,1)S(1)} %get-tuple-element.17.acc_hbm) | copy-start | bytes 12582916

commit v2 on v1

v2 whole, which is shorter than its diff:
```python
import functools

import jax
import jax.numpy as jnp
from jax import lax
from jax.experimental import pallas as pl
from jax.experimental.pallas import tpu as pltpu
from jax.sharding import PartitionSpec as P

QUERY_HEADS = 64
KEY_VALUE_HEADS = 8
HEAD_SIZE = 128
BLOCK_TOKENS = 128
LOCAL_BAND_SIZE = 4
PICKED_BLOCKS = 2
KEY_WIDTH = KEY_VALUE_HEADS * HEAD_SIZE
GROUP = QUERY_HEADS // KEY_VALUE_HEADS
ROWS = GROUP * BLOCK_TOKENS
PAIR = 2 * HEAD_SIZE
BLOCKS = 2

rope_base = 500000.0
masked_score = -1e30
score_factor = HEAD_SIZE ** (-0.5) * 1.4426950408889634

BAND_ROWS = 256
PICK_ROWS = 512
PICK_UNROLL = 2
PICK_AHEAD = 2

SMEM = pltpu.MemorySpace.SMEM


def rotary_tables(pos):
    half = HEAD_SIZE // 2
    freq = rope_base ** (-(jnp.arange(half, dtype=jnp.float32) * 2.0) / HEAD_SIZE)
    angle = pos.astype(jnp.float32)[:, None] * jnp.concatenate([freq, freq])[None, :]
    sign = jnp.where(jnp.arange(HEAD_SIZE) < half, -1.0, 1.0)
    return jnp.cos(angle), jnp.sin(angle) * sign[None, :]


def rotate(x, cosine, sine):
    wide = x.astype(jnp.float32)
    swapped = pltpu.roll(wide, HEAD_SIZE // 2, 1)
    return (wide * cosine + swapped * sine).astype(jnp.bfloat16)


def prep_kernel(limit, picks_ref, k_ref, v_ref, cos_ref, sin_ref, kr_ref, last_ref, table_ref, slot_ref, count_ref):
    shards = table_ref.shape[0]

    @pl.loop(0, shards)
    def _(i):
        count_ref[i] = 0
        for r in range(limit):
            table_ref[i, 0, r] = -1

    @pl.loop(0, BLOCKS * KEY_VALUE_HEADS)
    def _(i):
        b = i // KEY_VALUE_HEADS
        h = i % KEY_VALUE_HEADS
        for p in range(PICKED_BLOCKS):
            pick = picks_ref[b, p, h]
            slot_ref[i, p] = -1

            @pl.when(pick >= 0)
            def _():
                owner = pick // BLOCKS
                rank = jnp.minimum(count_ref[owner], limit - 1)
                count_ref[owner] = rank + 1
                table_ref[owner, 0, rank] = pick % BLOCKS * KEY_VALUE_HEADS + h
                slot_ref[i, p] = owner * limit + rank

    for b in range(BLOCKS):
        rows = slice(b * BLOCK_TOKENS, (b + 1) * BLOCK_TOKENS)
        cosine = cos_ref[rows, :]
        sine = sin_ref[rows, :]
        for h in range(KEY_VALUE_HEADS):
            cols = slice(h * HEAD_SIZE, (h + 1) * HEAD_SIZE)
            rotated = rotate(k_ref[rows, cols], cosine, sine)
            kr_ref[rows, cols] = rotated
            if b == BLOCKS - 1:
                last_ref[:, cols] = rotated
    last_ref[:, KEY_WIDTH:] = v_ref[(BLOCKS - 1) * BLOCK_TOKENS :, :]


def gather_kernel(wanted_ref, k_ref, v_ref, out_ref, sems):
    shards, _, limit = wanted_ref.shape

    def copies(i, r):
        entry = jnp.maximum(wanted_ref[i, 0, r], 0)
        rows = pl.ds(pl.multiple_of(entry // KEY_VALUE_HEADS * BLOCK_TOKENS, BLOCK_TOKENS), BLOCK_TOKENS)
        cols = pl.ds(pl.multiple_of(entry % KEY_VALUE_HEADS * HEAD_SIZE, HEAD_SIZE), HEAD_SIZE)
        return [
            pltpu.make_async_copy(src.at[rows, cols], out_ref.at[i, r, n], sems.at[n, i, r])
            for n, src in enumerate((k_ref, v_ref))
        ]

    @pl.loop(0, shards)
    def _(i):
        for r in range(limit):
            for copy in copies(i, r):
                copy.start()

    @pl.loop(0, shards)
    def _(i):
        for r in range(limit):
            for copy in copies(i, r):
                copy.wait()


def scores_of(query, key):
    return lax.dot_general(query, key, (((1,), (1,)), ((), ())), preferred_element_type=jnp.float32)


def summed(weight, value):
    both = jnp.concatenate([value, jnp.ones_like(value)], 1)
    out = jnp.dot(weight, both, preferred_element_type=jnp.float32)
    return out[:, :HEAD_SIZE], out[:, HEAD_SIZE:]


def band_kernel(b, me_ref, q_ref, cos_ref, sin_ref, nk_ref, nv_ref, k_ref, v_ref, *rest):
    far_refs = rest[:-3]
    qr_ref, acc_ref, lse_ref = rest[-3:]
    me = me_ref[0]
    row = lax.broadcasted_iota(jnp.int32, (BLOCK_TOKENS, BLOCK_TOKENS), 0)
    col = lax.broadcasted_iota(jnp.int32, (BLOCK_TOKENS, BLOCK_TOKENS), 1)
    causal = jnp.concatenate([col <= row] * (BAND_ROWS // BLOCK_TOKENS), 0)
    edge = (LOCAL_BAND_SIZE - 1) * BLOCK_TOKENS
    own = (b + 1) * BLOCK_TOKENS
    rows = slice(b * BLOCK_TOKENS, (b + 1) * BLOCK_TOKENS)

    def attend(start, h):
        at_key = pl.ds(pl.multiple_of(h * HEAD_SIZE, HEAD_SIZE), HEAD_SIZE)
        at_value = pl.ds(pl.multiple_of(KEY_WIDTH + h * HEAD_SIZE, HEAD_SIZE), HEAD_SIZE)
        keys = [nk_ref[:, at_key], k_ref[:own, at_key]]
        values = [nv_ref[:, at_key], v_ref[:own, at_key]]
        if far_refs:
            even_ref, odd_ref = far_refs
            odd = me % 2 == 1
            keys = [jnp.where(odd, odd_ref[:, at_key], even_ref[:, at_key])] + keys
            values = [jnp.where(odd, odd_ref[:, at_value], even_ref[:, at_value])] + values
        key = jnp.concatenate(keys, 0)
        value = jnp.concatenate(values, 0)
        query = q_ref[rows, pl.ds(pl.multiple_of(h * ROWS, ROWS), ROWS)]
        for first in range(0, ROWS, BAND_ROWS):
            part = slice(first, first + BAND_ROWS)
            rotated = jnp.concatenate(
                [
                    rotate(query[:, at : at + HEAD_SIZE], cos_ref[rows, :], sin_ref[rows, :])
                    for at in range(first, first + BAND_ROWS, HEAD_SIZE)
                ],
                0,
            )
            qr_ref[h, part, :] = rotated
            score = scores_of(rotated, key)
            before = score[:, :edge]
            if start:
                oldest = (me * BLOCKS + b - (LOCAL_BAND_SIZE - 1)) * BLOCK_TOKENS
                index = oldest + lax.broadcasted_iota(jnp.int32, before.shape, 1)
                before = jnp.where(index >= 0, before, masked_score)
            score = jnp.concatenate([before, jnp.where(causal, score[:, edge:], masked_score)], 1)
            top = jnp.max(score, -1, keepdims=True) * score_factor
            weight = jnp.exp2(score * score_factor - top)
            out, total = summed(weight.astype(jnp.bfloat16), value)
            acc_ref[h, part, :] = (out / total).astype(acc_ref.dtype)
            lse_ref[h, part, :] = jnp.log2(total) + top

    early = me * BLOCKS + b < LOCAL_BAND_SIZE - 1

    @pl.when(early)
    def _():
        pl.loop(0, KEY_VALUE_HEADS)(functools.partial(attend, True))

    @pl.when(jnp.logical_not(early))
    def _():
        pl.loop(0, KEY_VALUE_HEADS)(functools.partial(attend, False))


def picks_kernel(slot_ref, landed_hbm, *rest):
    band_hbm = rest[: 3 * BLOCKS]
    out_hbm, q_ref, piece_ref, acc_ref, lse_ref, out_ref, ins, outs = rest[3 * BLOCKS :]
    rounds = KEY_VALUE_HEADS // PICK_UNROLL

    def loads(b, h):
        i = b * KEY_VALUE_HEADS + h
        pairs = [(landed_hbm.at[jnp.maximum(slot_ref[i, p], 0)], piece_ref.at[i, p]) for p in range(PICKED_BLOCKS)]
        pairs += [(src.at[h], dst.at[i]) for src, dst in zip(band_hbm[3 * b : 3 * b + 3], (q_ref, acc_ref, lse_ref))]
        return [pltpu.make_async_copy(src, dst, ins.at[i, n]) for n, (src, dst) in enumerate(pairs)]

    def store(b, h):
        i = b * KEY_VALUE_HEADS + h
        rows = pl.ds(b * BLOCK_TOKENS, BLOCK_TOKENS)
        cols = pl.ds(pl.multiple_of(h * ROWS, ROWS), ROWS)
        return pltpu.make_async_copy(out_ref.at[i], out_hbm.at[rows, cols], outs.at[i])

    def start_round(b, j):
        for u in range(PICK_UNROLL):
            for copy in loads(b, j * PICK_UNROLL + u):
                copy.start()

    def step(i):
        bias = jnp.where(slot_ref[i, 0] >= 0, 0.0, masked_score)
        key = jnp.concatenate([piece_ref[i, p, 0] for p in range(PICKED_BLOCKS)], 0)
        value = jnp.concatenate([piece_ref[i, p, 1] for p in range(PICKED_BLOCKS)], 0)
        for first in range(0, ROWS, PICK_ROWS):
            part = slice(first, first + PICK_ROWS)
            score = scores_of(q_ref[i, part, :], key)
            old = lse_ref[i, part, :]
            best = jnp.broadcast_to(jnp.max(score, -1, keepdims=True) * score_factor, old.shape) + bias
            top = jnp.maximum(best, old)
            shift = top - bias
            weight = jnp.exp2(score * score_factor - jnp.concatenate([shift] * PICKED_BLOCKS, 1))
            fade = jnp.exp2(old - top)
            out, total = summed(weight.astype(jnp.bfloat16), value)
            out = out + acc_ref[i, part, :].astype(jnp.float32) * fade
            result = (out / (total + fade)).astype(out_ref.dtype)
            for g in range(PICK_ROWS // BLOCK_TOKENS):
                at = slice(g * BLOCK_TOKENS, (g + 1) * BLOCK_TOKENS)
                out_ref[i, :, first + g * HEAD_SIZE : first + (g + 1) * HEAD_SIZE] = result[at]

    for j in range(PICK_AHEAD):
        start_round(0, j)

    for b in range(BLOCKS):

        @pl.loop(0, rounds)
        def _(j):
            @pl.when(j + PICK_AHEAD < rounds)
            def _():
                start_round(b, j + PICK_AHEAD)

            if b + 1 < BLOCKS:

                @pl.when(j + PICK_AHEAD >= rounds)
                def _():
                    start_round(b + 1, j + PICK_AHEAD - rounds)

            for u in range(PICK_UNROLL):
                for copy in loads(b, j * PICK_UNROLL + u):
                    copy.wait()

            for u in range(PICK_UNROLL):
                h = j * PICK_UNROLL + u
                step(b * KEY_VALUE_HEADS + h)
                store(b, h).start()

    for b in range(BLOCKS):
        for h in range(KEY_VALUE_HEADS):
            store(b, h).wait()


def shards(queries, keys, values, positions, picks):
    tokens = queries.shape[0]
    window = lax.axis_size("ctx")
    limit = max(1, BLOCKS * KEY_VALUE_HEADS * PICKED_BLOCKS // window)
    me = lax.axis_index("ctx").astype(jnp.int32).reshape(1)
    cosine, sine = rotary_tables(positions)
    bf16 = jnp.bfloat16
    vmem = pl.BlockSpec(memory_space=pltpu.MemorySpace.VMEM)
    smem = pl.BlockSpec(memory_space=SMEM)
    hbm = pl.BlockSpec(memory_space=pl.ANY)

    near_v = lax.ppermute(values, "ctx", [(i - 1, i) for i in range(1, window)])
    rotated_keys, last, table, slot = pl.pallas_call(
        functools.partial(prep_kernel, limit),
        out_shape=(
            jax.ShapeDtypeStruct((tokens, KEY_WIDTH), bf16),
            jax.ShapeDtypeStruct((BLOCK_TOKENS, 2 * KEY_WIDTH), bf16),
            jax.ShapeDtypeStruct((window, 1, limit), jnp.int32),
            jax.ShapeDtypeStruct((BLOCKS * KEY_VALUE_HEADS, PICKED_BLOCKS), jnp.int32),
        ),
        in_specs=[smem, vmem, vmem, vmem, vmem],
        out_specs=(vmem, vmem, smem, smem),
        scratch_shapes=[pltpu.SMEM((window,), jnp.int32)],
        name="prep",
    )(picks.transpose(0, 2, 1), keys, values, cosine, sine)

    near_k = lax.ppermute(rotated_keys, "ctx", [(i - 1, i) for i in range(1, window)])
    wanted = lax.all_to_all(table, "ctx", split_axis=0, concat_axis=0, tiled=True)
    wanted, last, near_k, near_v = lax.optimization_barrier((wanted, last, near_k, near_v))
    far_even = lax.ppermute(last, "ctx", [(i - 2, i) for i in range(2, window, 2)])

    answer = pl.pallas_call(
        gather_kernel,
        out_shape=jax.ShapeDtypeStruct((window, limit, 2, BLOCK_TOKENS, HEAD_SIZE), bf16),
        in_specs=[smem, vmem, vmem],
        out_specs=hbm,
        scratch_shapes=[pltpu.SemaphoreType.DMA((2, window, limit))],
        cost_estimate=pl.CostEstimate(flops=0, bytes_accessed=60 << 20, transcendentals=0),
        name="gather",
    )(wanted, rotated_keys, values)
    landed = lax.all_to_all(answer, "ctx", split_axis=0, concat_axis=0, tiled=True)
    landed = landed.reshape(window * limit, 2, BLOCK_TOKENS, HEAD_SIZE)

    band_flops = 4 * BLOCKS * QUERY_HEADS * BLOCK_TOKENS * LOCAL_BAND_SIZE * BLOCK_TOKENS * HEAD_SIZE
    full = (KEY_VALUE_HEADS, ROWS, HEAD_SIZE)

    def band(b, weight, *far):
        return pl.pallas_call(
            functools.partial(band_kernel, b),
            out_shape=(
                jax.ShapeDtypeStruct(full, bf16),
                jax.ShapeDtypeStruct(full, bf16),
                jax.ShapeDtypeStruct(full, jnp.float32),
            ),
            in_specs=[smem] + [vmem] * (7 + len(far)),
            out_specs=(vmem,) * 3,
            cost_estimate=pl.CostEstimate(flops=weight * band_flops, bytes_accessed=8 << 20, transcendentals=1 << 22),
            compiler_params=pltpu.CompilerParams(vmem_limit_bytes=30 << 20),
            name="band",
        )(me, queries, cosine, sine, near_k, near_v, rotated_keys, values, *far)

    second = band(1, 50)
    edge_k, edge_v, _ = lax.optimization_barrier((near_k, near_v, second[2]))
    edge = jnp.concatenate([edge_k[tokens - BLOCK_TOKENS :], edge_v[tokens - BLOCK_TOKENS :]], 1)
    far_odd = lax.ppermute(edge, "ctx", [(i - 1, i) for i in range(1, window, 2)])
    first = band(0, 1, far_even, far_odd)

    count = BLOCKS * KEY_VALUE_HEADS
    narrow = (count, ROWS, HEAD_SIZE)
    return pl.pallas_call(
        picks_kernel,
        out_shape=jax.ShapeDtypeStruct((tokens, QUERY_HEADS * HEAD_SIZE), bf16),
        in_specs=[smem] + [hbm] * (1 + 3 * BLOCKS),
        out_specs=hbm,
        scratch_shapes=[
            pltpu.VMEM(narrow, bf16),
            pltpu.VMEM((count, PICKED_BLOCKS, 2, BLOCK_TOKENS, HEAD_SIZE), bf16),
            pltpu.VMEM(narrow, bf16),
            pltpu.VMEM(narrow, jnp.float32),
            pltpu.VMEM((count, BLOCK_TOKENS, ROWS), bf16),
            pltpu.SemaphoreType.DMA((count, PICKED_BLOCKS + 3)),
            pltpu.SemaphoreType.DMA((count,)),
        ],
        cost_estimate=pl.CostEstimate(flops=2 * band_flops, bytes_accessed=16 << 20, transcendentals=1 << 22),
        compiler_params=pltpu.CompilerParams(vmem_limit_bytes=58 << 20),
        name="picks",
    )(slot, landed, *first, *second)


def solution(mesh):
    return jax.shard_map(
        shards,
        mesh=mesh,
        in_specs=(
            P(("groups", "ctx"), None),
            P(("groups", "ctx"), None),
            P(("groups", "ctx"), None),
            P(("groups", "ctx")),
            P(("groups", "ctx"), None, None),
        ),
        out_specs=P(("groups", "ctx"), None),
        check_vma=False,
    )
```

time: 106 us -> 94.5 us (0.89)
  waiting for transfers between devices: 38.6 us -> 20.1 us
  starting transfers between devices: 18.5 us -> 22.6 us
  Pallas kernels: 35.3 us -> 38.8 us
  local copies, waits for them, and re-layouts: 11.3 us -> 10.2 us
    all_to_all x1, waiting for transfers between devices: 15.8 us -> 3.73 us  [shards(): lax.all_to_all(table, 'ctx', split_axis=0, concat_axis=0, tiled=True)]
    all_to_all x1, waiting for transfers between devices: 22.8 us -> 13.9 us  [shards(): lax.all_to_all(answer, 'ctx', split_axis=0, concat_axis=0, tiled=True)]
    pallas_call x1 -> x2, Pallas kernels: 15.3 us -> 19.5 us  [band(): pl.pallas_call(functools.partial(band_kernel, b), out_shape=(jax.ShapeDty...]
    ppermute x2 -> x4, waiting for transfers between devices: 0.01 us -> 2.49 us  [the longest x1 2.48 us: shards(): lax.ppermute(edge, 'ctx', [(i - 1, i) for i in range(1, window, 2)])]
    all_to_all x1, starting transfers between devices: 6.51 us -> 8.8 us  [shards(): lax.all_to_all(answer, 'ctx', split_axis=0, concat_axis=0, tiled=True)]
    ppermute x2 -> x4, starting transfers between devices: 6.99 us -> 8.42 us  [the longest x1 3.73 us: shards(): near_v = lax.ppermute(values, 'ctx', [(i - 1, i) for i in range(1, window)])]
    mul x0 -> x1, other arithmetic: none -> 1.25 us  [rotary_tables(): return (jnp.cos(angle), jnp.sin(angle) * sign[None, :])]
    unnamed x17 -> x24, local copies, waits for them, and re-layouts: 11.3 us -> 10.1 us
  transfers between devices with their start and end apart: 4 -> 6, of which waited for: 2 -> 3; matrix products, arithmetic and copies ran while one was open for 0% -> 2% of each run, Pallas kernels for 17% -> 28%
where the time goes in v2:
time: 94.5 us; the launch traced here: 94 us
  Pallas kernels  38.8 us (41%)
  starting transfers between devices  22.6 us (24%)
  waiting for transfers between devices  20.1 us (21%)
  local copies, waits for them, and re-layouts  10.2 us (11%)
  other arithmetic  2.06 us (2%)
    pallas_call x2, Pallas kernels, band(): pl.pallas_call(functools.partial(band_kernel, b), out_shape=(jax.ShapeDty...  19.5 us
    all_to_all x1, waiting for transfers between devices, shards(): lax.all_to_all(answer, 'ctx', split_axis=0, concat_axis=0, tiled=True)  13.9 us
    pallas_call x1, Pallas kernels, shards(): pl.pallas_call(picks_kernel, out_shape=jax.ShapeDtypeStruct((tokens, QUER...  12.9 us
    unnamed x24, local copies, waits for them, and re-layouts  10.1 us
    all_to_all x1, starting transfers between devices, shards(): lax.all_to_all(answer, 'ctx', split_axis=0, concat_axis=0, tiled=True)  8.8 us
    all_to_all x1, starting transfers between devices, shards(): lax.all_to_all(table, 'ctx', split_axis=0, concat_axis=0, tiled=True)  5.41 us
    ppermute x1, starting transfers between devices, shards(): near_v = lax.ppermute(values, 'ctx', [(i - 1, i) for i in range(1, window)])  3.73 us
    all_to_all x1, waiting for transfers between devices, shards(): lax.all_to_all(table, 'ctx', split_axis=0, concat_axis=0, tiled=True)  3.73 us
  transfers between devices with their start and end apart: 6, of which 3 were waited for; matrix products, arithmetic and copies ran while one was open for 2% of the time, Pallas kernels for 28%

profile of v2, /device:TPU:15, one launch (start us, length us, event | category | flops | bytes accessed | tf_op | source)
XLA Modules:
  0.0 94.0 jit_solution(7823803410690710141)
XLA Ops:
  0.0 3.7 %collective-permute-start.1 = (bf16[256,1024]{1,0:T(8,128)(2,1)}, bf16[256,1024]{1,0:T(8,128)(2,1)S(1)}, u32[]{:S(2)}, u32[]{:S(2)}) collective-permute-start(bf16[256,1024]{1,0:T(8,128)(2,1)} %v_ref.7), channel_id=1, source_target_pairs={{0,1},{1,2},{2,3},{3,4},{4,5},{5,6},{6,7},{7,8},{8,9},{9,10},{10,1... | collective-permute-start | bytes 1572872 | tf_op jit(solution)/shard_map/ppermute | solution.py:263
  3.8 0.1 compare_select_fusion
  3.8 0.7 convert_element_type.3
  4.5 1.2 %fusion = (f32[256,128]{1,0:T(8,128)}, f32[256,128]{1,0:T(8,128)}) fusion(f32[128]{0:T(128)S(1)} %get-tuple-element.39, f32[128]{0:T(128)S(1)} %get-tuple-element.40, f32[256]{0:T(256)S(1)} %convert_element_type.3), kind=kLoop, calls=%fused_computation.3 | loop fusion | flops 65536 | bytes 264192 | tf_op jit(solution)/shard_map/mul | solution.py:39
  5.8 3.3 %prep.1 = (bf16[256,1024]{1,0:T(8,128)(2,1)}, bf16[128,2048]{1,0:T(8,128)(2,1)}, s32[16,1,2]{2,1,0:T(1,128)}, s32[16,2]{1,0:T(8,128)}) custom-call(s32[2,2,8]{2,1,0:T(2,128)} %bitcast.3, bf16[256,1024]{1,0:T(8,128)(2,1)} %k_ref.1, bf16[256,1024]{1,0:T(8,128)(2,1)} %v_ref.7, f32[256,128]{1,0:T(8,128)} %get-tuple-element.38.cos_ref, ...), custom_call_target="tpu_custom_call" | custom-call | tf_op jit(solution)/shard_map/prep/pallas_call | solution.py:264
  9.1 1.9 %collective-permute-start = (bf16[256,1024]{1,0:T(8,128)(2,1)}, bf16[256,1024]{1,0:T(8,128)(2,1)S(1)}, u32[]{:S(2)}, u32[]{:S(2)}) collective-permute-start(bf16[256,1024]{1,0:T(8,128)(2,1)} %get-tuple-element.24.k_ref), channel_id=1, source_target_pairs={{0,1},{1,2},{2,3},{3,4},{4,5},{5,6},{6,7},{7,8},{8,9},{9,10},{10,1... | collective-permute-start | bytes 1572872 | tf_op jit(solution)/shard_map/ppermute | solution.py:278
  11.0 5.4 %all-to-all-start = ((s32[16,1,2]{2,1,0:T(1,128)}), s32[16,1,2]{2,1,0:T(1,128)S(1)}, u32[]{:S(2)}, u32[]{:S(2)}) async-start(s32[16,1,2]{2,1,0:T(1,128)} %get-tuple-element.22), calls=%async_computation | async-start | bytes 16384 | tf_op jit(solution)/shard_map/all_to_all | solution.py:279
  16.4 3.7 %all-to-all-done.wanted_ref = s32[16,1,2]{2,1,0:T(1,128)S(1)} async-done(((s32[16,1,2]{2,1,0:T(1,128)}), s32[16,1,2]{2,1,0:T(1,128)S(1)}, u32[]{:S(2)}, u32[]{:S(2)}) %all-to-all-start) | async-done | bytes 160 | tf_op jit(solution)/shard_map/all_to_all | solution.py:279
  20.1 0.0 copy-start.11
  20.1 0.0 collective-permute-done.1.nv_ref
  20.1 0.0 collective-permute-done.nk_ref
  20.1 1.5 %collective-permute-start.2 = (bf16[128,2048]{1,0:T(8,128)(2,1)}, bf16[128,2048]{1,0:T(8,128)(2,1)}, u32[]{:S(2)}, u32[]{:S(2)}) collective-permute-start(bf16[128,2048]{1,0:T(8,128)(2,1)} %get-tuple-element.28), channel_id=1, source_target_pairs={{0,2},{2,4},{4,6},{6,8},{8,10},{10,12},{12,14},{16,18},{18,20},{20... | collective-permute-start | bytes 1572872 | tf_op jit(solution)/shard_map/ppermute | solution.py:281
  21.6 0.0 copy-done.11
  21.6 3.1 %gather.1 = bf16[16,2,2,128,128]{4,3,2,1,0:T(8,128)(2,1)} custom-call(s32[16,1,2]{2,1,0:T(1,128)} %copy-done.11, bf16[256,1024]{1,0:T(8,128)(2,1)} %get-tuple-element.24.k_ref, bf16[256,1024]{1,0:T(8,128)(2,1)} %v_ref.7), custom_call_target="tpu_custom_call" | custom-call | bytes 62914560 | tf_op jit(solution)/shard_map/gather/pallas_call | solution.py:283
  24.7 0.0 copy-start
  24.7 0.0 copy-start.1
  24.7 0.0 copy-start.2
  24.7 0.0 copy-start.3
  24.7 8.8 %all-to-all-start.1 = ((bf16[16,2,2,128,128]{4,3,2,1,0:T(8,128)(2,1)}), bf16[16,2,2,128,128]{4,3,2,1,0:T(8,128)(2,1)}, u32[]{:S(2)}, u32[]{:S(2)}) async-start(bf16[16,2,2,128,128]{4,3,2,1,0:T(8,128)(2,1)} %gather.1), calls=%async_computation.1 | async-start | bytes 4194304 | tf_op jit(solution)/shard_map/all_to_all | solution.py:292
  33.5 0.0 copy-done
  33.5 0.0 copy-done.1
  33.6 0.0 copy-done.2
  33.6 0.0 copy-done.3
  33.6 0.0 copy-start.4
  33.6 2.2 %copy-done.4 = bf16[256,8192]{1,0:T(8,128)(2,1)S(1)} copy-done((bf16[256,8192]{1,0:T(8,128)(2,1)S(1)}, bf16[256,8192]{1,0:T(8,128)(2,1)}, u32[]{:S(2)}) %copy-start.4) | copy-done | bytes 4194328
  35.8 9.2 %band.2 = (bf16[8,1024,128]{2,1,0:T(8,128)(2,1)S(1)}, bf16[8,1024,128]{2,1,0:T(8,128)(2,1)S(1)}, f32[8,1024,128]{2,1,0:T(8,128)S(1)}) custom-call(s32[1]{0:T(128)} %bitcast.2.me_ref, bf16[256,8192]{1,0:T(8,128)(2,1)S(1)} %copy-done.4, f32[256,128]{1,0:T(8,128)S(1)} %copy-done.2, f32[256,128]{1,0:T(8,128)S(1)} %copy-done.1, ...), custom_call_target="tpu_custom_call" | custom-call | flops 214748364800 | bytes 8388608 | tf_op jit(solution)/shard_map/band/pallas_call | solution.py:299
  45.0 0.0 copy-start.6
  45.0 1.9 %copy-done.6 = f32[8,1024,128]{2,1,0:T(8,128)} copy-done((f32[8,1024,128]{2,1,0:T(8,128)}, f32[8,1024,128]{2,1,0:T(8,128)S(1)}, u32[]{:S(2)}) %copy-start.6) | copy-done | bytes 4194328
  47.0 0.0 copy-start.9
  47.0 1.4 %copy-done.9 = bf16[8,1024,128]{2,1,0:T(8,128)(2,1)} copy-done((bf16[8,1024,128]{2,1,0:T(8,128)(2,1)}, bf16[8,1024,128]{2,1,0:T(8,128)(2,1)S(1)}, u32[]{:S(2)}) %copy-start.9) | copy-done | bytes 2097176
  48.3 0.0 copy-start.10
  48.4 1.3 %collective-permute-start.3 = (bf16[128,2048]{1,0:T(8,128)(2,1)S(1)}, bf16[128,2048]{1,0:T(8,128)(2,1)S(1)}, u32[]{:S(2)}, u32[]{:S(2)}) collective-permute-start(bf16[128,2048]{1,0:T(8,128)(2,1)S(1)} %pad_maximum_fusion), channel_id=1, source_target_pairs={{0,1},{2,3},{4,5},{6,7},{8,9},{10,11},{12,13},{14,15},{16,17},{18,... | collective-permute-start | bytes 1572872 | tf_op jit(solution)/shard_map/ppermute | solution.py:316
  49.7 0.0 collective-permute-done.2.rest_0_
  49.7 0.0 copy-done.10
  49.7 2.5 %collective-permute-done.3.rest_1_ = bf16[128,2048]{1,0:T(8,128)(2,1)S(1)} collective-permute-done((bf16[128,2048]{1,0:T(8,128)(2,1)S(1)}, bf16[128,2048]{1,0:T(8,128)(2,1)S(1)}, u32[]{:S(2)}, u32[]{:S(2)}) %collective-permute-start.3) | collective-permute-done | bytes 524320 | tf_op jit(solution)/shard_map/ppermute | solution.py:316
  52.2 10.3 %band.3 = (bf16[8,1024,128]{2,1,0:T(8,128)(2,1)S(1)}, bf16[8,1024,128]{2,1,0:T(8,128)(2,1)S(1)}, f32[8,1024,128]{2,1,0:T(8,128)S(1)}) custom-call(s32[1]{0:T(128)} %bitcast.2.me_ref, bf16[256,8192]{1,0:T(8,128)(2,1)S(1)} %copy-done.4, f32[256,128]{1,0:T(8,128)S(1)} %copy-done.2, f32[256,128]{1,0:T(8,128)S(1)} %copy-done.1, ...), custom_call_target="tpu_custom_call" | custom-call | flops 4294967296 | bytes 8388608 | tf_op jit(solution)/shard_map/band/pallas_call | solution.py:299
  62.5 0.0 copy-start.5
  62.5 2.0 %copy-done.5 = f32[8,1024,128]{2,1,0:T(8,128)} copy-done((f32[8,1024,128]{2,1,0:T(8,128)}, f32[8,1024,128]{2,1,0:T(8,128)S(1)}, u32[]{:S(2)}) %copy-start.5) | copy-done | bytes 4194328
  64.5 0.0 copy-start.7
  64.5 1.3 %copy-done.7 = bf16[8,1024,128]{2,1,0:T(8,128)(2,1)} copy-done((bf16[8,1024,128]{2,1,0:T(8,128)(2,1)}, bf16[8,1024,128]{2,1,0:T(8,128)(2,1)S(1)}, u32[]{:S(2)}) %copy-start.7) | copy-done | bytes 2097176
  65.8 0.0 copy-start.8
  65.8 1.3 %copy-done.8 = bf16[8,1024,128]{2,1,0:T(8,128)(2,1)} copy-done((bf16[8,1024,128]{2,1,0:T(8,128)(2,1)}, bf16[8,1024,128]{2,1,0:T(8,128)(2,1)S(1)}, u32[]{:S(2)}) %copy-start.8) | copy-done | bytes 2097176
  67.2 13.9 %all-to-all-done.1 = bf16[16,2,2,128,128]{4,3,2,1,0:T(8,128)(2,1)} async-done(((bf16[16,2,2,128,128]{4,3,2,1,0:T(8,128)(2,1)}), bf16[16,2,2,128,128]{4,3,2,1,0:T(8,128)(2,1)}, u32[]{:S(2)}, u32[]{:S(2)}) %all-to-all-start.1) | async-done | bytes 2097184 | tf_op jit(solution)/shard_map/all_to_all | solution.py:292
  81.1 12.9 %picks.1 = bf16[256,8192]{1,0:T(8,128)(2,1)} custom-call(s32[16,2]{1,0:T(8,128)} %get-tuple-element.21.slot_ref, bf16[32,2,128,128]{3,2,1,0:T(8,128)(2,1)} %bitcast.1.landed_hbm, bf16[8,1024,128]{2,1,0:T(8,128)(2,1)} %copy-done.7, bf16[8,1024,128]{2,1,0:T(8,128)(2,1)} %copy-done.8, f32[8,1024,128]{2,1,0:T(8,128)} %copy-done.5, ...), custom_call_target="tpu_custom_call" | custom-call | flops 8589934592 | bytes 16777216 | tf_op jit(solution)/shard_map/picks/pallas_call | solution.py:321
  (4 shorter events, 0.1 us)
Async XLA Ops:
  0.0 20.1 %collective-permute-start.1 = (bf16[256,1024]{1,0:T(8,128)(2,1)}, bf16[256,1024]{1,0:T(8,128)(2,1)S(1)}, u32[]{:S(2)}, u32[]{:S(2)}) collective-permute-start(bf16[256,1024]{1,0:T(8,128)(2,1)} %v_ref.7), channel_id=1, source_target_pairs={{0,1},{1,2},{2,3},{3,4},{4,5},{5,6},{6,7},{7,8},{8,9},{9,10},{10,1... | collective-permute-start | bytes 1572872 | tf_op jit(solution)/shard_map/ppermute | solution.py:263
  9.1 11.1 %collective-permute-start = (bf16[256,1024]{1,0:T(8,128)(2,1)}, bf16[256,1024]{1,0:T(8,128)(2,1)S(1)}, u32[]{:S(2)}, u32[]{:S(2)}) collective-permute-start(bf16[256,1024]{1,0:T(8,128)(2,1)} %get-tuple-element.24.k_ref), channel_id=1, source_target_pairs={{0,1},{1,2},{2,3},{3,4},{4,5},{5,6},{6,7},{7,8},{8,9},{9,10},{10,1... | collective-permute-start | bytes 1572872 | tf_op jit(solution)/shard_map/ppermute | solution.py:278
  11.0 9.1 %all-to-all-start = ((s32[16,1,2]{2,1,0:T(1,128)}), s32[16,1,2]{2,1,0:T(1,128)S(1)}, u32[]{:S(2)}, u32[]{:S(2)}) async-start(s32[16,1,2]{2,1,0:T(1,128)} %get-tuple-element.22), calls=%async_computation | async-start | bytes 16384 | tf_op jit(solution)/shard_map/all_to_all | solution.py:279
  20.1 1.5 %copy-start.11 = (s32[16,1,2]{2,1,0:T(1,128)}, s32[16,1,2]{2,1,0:T(1,128)S(1)}, u32[]{:S(2)}) copy-start(s32[16,1,2]{2,1,0:T(1,128)S(1)} %all-to-all-done.wanted_ref) | copy-start | bytes 388
  20.1 29.6 %collective-permute-start.2 = (bf16[128,2048]{1,0:T(8,128)(2,1)}, bf16[128,2048]{1,0:T(8,128)(2,1)}, u32[]{:S(2)}, u32[]{:S(2)}) collective-permute-start(bf16[128,2048]{1,0:T(8,128)(2,1)} %get-tuple-element.28), channel_id=1, source_target_pairs={{0,2},{2,4},{4,6},{6,8},{8,10},{10,12},{12,14},{16,18},{18,20},{20... | collective-permute-start | bytes 1572872 | tf_op jit(solution)/shard_map/ppermute | solution.py:281
  24.7 8.8 %copy-start = (bf16[256,1024]{1,0:T(8,128)(2,1)S(1)}, bf16[256,1024]{1,0:T(8,128)(2,1)}, u32[]{:S(2)}) copy-start(bf16[256,1024]{1,0:T(8,128)(2,1)} %v_ref.7) | copy-start | bytes 1572868
  24.7 8.8 %copy-start.1 = (f32[256,128]{1,0:T(8,128)S(1)}, f32[256,128]{1,0:T(8,128)}, u32[]{:S(2)}) copy-start(f32[256,128]{1,0:T(8,128)} %get-tuple-element.37.sin_ref) | copy-start | bytes 393220
  24.7 8.8 %copy-start.2 = (f32[256,128]{1,0:T(8,128)S(1)}, f32[256,128]{1,0:T(8,128)}, u32[]{:S(2)}) copy-start(f32[256,128]{1,0:T(8,128)} %get-tuple-element.38.cos_ref) | copy-start | bytes 393220
  24.7 8.8 %copy-start.3 = (bf16[256,1024]{1,0:T(8,128)(2,1)S(1)}, bf16[256,1024]{1,0:T(8,128)(2,1)}, u32[]{:S(2)}) copy-start(bf16[256,1024]{1,0:T(8,128)(2,1)} %get-tuple-element.24.k_ref) | copy-start | bytes 1572868
  24.7 56.3 %all-to-all-start.1 = ((bf16[16,2,2,128,128]{4,3,2,1,0:T(8,128)(2,1)}), bf16[16,2,2,128,128]{4,3,2,1,0:T(8,128)(2,1)}, u32[]{:S(2)}, u32[]{:S(2)}) async-start(bf16[16,2,2,128,128]{4,3,2,1,0:T(8,128)(2,1)} %gather.1), calls=%async_computation.1 | async-start | bytes 4194304 | tf_op jit(solution)/shard_map/all_to_all | solution.py:292
  33.6 2.2 %copy-start.4 = (bf16[256,8192]{1,0:T(8,128)(2,1)S(1)}, bf16[256,8192]{1,0:T(8,128)(2,1)}, u32[]{:S(2)}) copy-start(bf16[256,8192]{1,0:T(8,128)(2,1)} %q_ref.3) | copy-start | bytes 12582916
  45.0 1.9 %copy-start.6 = (f32[8,1024,128]{2,1,0:T(8,128)}, f32[8,1024,128]{2,1,0:T(8,128)S(1)}, u32[]{:S(2)}) copy-start(f32[8,1024,128]{2,1,0:T(8,128)S(1)} %get-tuple-element.29.rest_5_) | copy-start | bytes 12582916
  47.0 1.4 %copy-start.9 = (bf16[8,1024,128]{2,1,0:T(8,128)(2,1)}, bf16[8,1024,128]{2,1,0:T(8,128)(2,1)S(1)}, u32[]{:S(2)}) copy-start(bf16[8,1024,128]{2,1,0:T(8,128)(2,1)S(1)} %get-tuple-element.35.rest_3_) | copy-start | bytes 6291460
  48.3 1.4 %copy-start.10 = (bf16[8,1024,128]{2,1,0:T(8,128)(2,1)}, bf16[8,1024,128]{2,1,0:T(8,128)(2,1)S(1)}, u32[]{:S(2)}) copy-start(bf16[8,1024,128]{2,1,0:T(8,128)(2,1)S(1)} %get-tuple-element.36.rest_4_) | copy-start | bytes 6291460
  48.4 3.8 %collective-permute-start.3 = (bf16[128,2048]{1,0:T(8,128)(2,1)S(1)}, bf16[128,2048]{1,0:T(8,128)(2,1)S(1)}, u32[]{:S(2)}, u32[]{:S(2)}) collective-permute-start(bf16[128,2048]{1,0:T(8,128)(2,1)S(1)} %pad_maximum_fusion), channel_id=1, source_target_pairs={{0,1},{2,3},{4,5},{6,7},{8,9},{10,11},{12,13},{14,15},{16,17},{18,... | collective-permute-start | bytes 1572872 | tf_op jit(solution)/shard_map/ppermute | solution.py:316
  62.5 2.0 %copy-start.5 = (f32[8,1024,128]{2,1,0:T(8,128)}, f32[8,1024,128]{2,1,0:T(8,128)S(1)}, u32[]{:S(2)}) copy-start(f32[8,1024,128]{2,1,0:T(8,128)S(1)} %get-tuple-element.34.rest_2_) | copy-start | bytes 12582916
  64.5 1.3 %copy-start.7 = (bf16[8,1024,128]{2,1,0:T(8,128)(2,1)}, bf16[8,1024,128]{2,1,0:T(8,128)(2,1)S(1)}, u32[]{:S(2)}) copy-start(bf16[8,1024,128]{2,1,0:T(8,128)(2,1)S(1)} %get-tuple-element.32.rest_0_) | copy-start | bytes 6291460
  65.8 1.3 %copy-start.8 = (bf16[8,1024,128]{2,1,0:T(8,128)(2,1)}, bf16[8,1024,128]{2,1,0:T(8,128)(2,1)S(1)}, u32[]{:S(2)}) copy-start(bf16[8,1024,128]{2,1,0:T(8,128)(2,1)S(1)} %get-tuple-element.33.rest_1_) | copy-start | bytes 6291460

commit v3 on v2

--- a/solution.py
+++ b/solution.py
@@ -23,9 +23,11 @@
 masked_score = -1e30
 score_factor = HEAD_SIZE ** (-0.5) * 1.4426950408889634
 
+PARTS = 3
+
 BAND_ROWS = 256
 PICK_ROWS = 512
-PICK_UNROLL = 2
+PICK_UNROLL = 4
 PICK_AHEAD = 2
 
 SMEM = pltpu.MemorySpace.SMEM
@@ -120,7 +122,9 @@
 
 def band_kernel(b, me_ref, q_ref, cos_ref, sin_ref, nk_ref, nv_ref, k_ref, v_ref, *rest):
     far_refs = rest[:-3]
-    qr_ref, acc_ref, lse_ref = rest[-3:]
+    qr_ref, acc_ref, sums_ref = rest[-3:]
+    lane = lax.broadcasted_iota(jnp.int32, (BAND_ROWS, HEAD_SIZE), 1)
+    sums_ref[...] = jnp.zeros_like(sums_ref)
     me = me_ref[0]
     row = lax.broadcasted_iota(jnp.int32, (BLOCK_TOKENS, BLOCK_TOKENS), 0)
     col = lax.broadcasted_iota(jnp.int32, (BLOCK_TOKENS, BLOCK_TOKENS), 1)
@@ -163,7 +167,13 @@
             weight = jnp.exp2(score * score_factor - top)
             out, total = summed(weight.astype(jnp.bfloat16), value)
             acc_ref[h, part, :] = (out / total).astype(acc_ref.dtype)
-            lse_ref[h, part, :] = jnp.log2(total) + top
+            left = (jnp.log2(total) + top) * (1.0 / score_factor)
+            sums = sums_ref[part, :].astype(jnp.float32)
+            for n in range(PARTS):
+                addend = left.astype(jnp.bfloat16).astype(jnp.float32)
+                sums = jnp.where(lane == PARTS * h + n, addend, sums)
+                left = left - addend
+            sums_ref[part, :] = sums.astype(sums_ref.dtype)
 
     early = me * BLOCKS + b < LOCAL_BAND_SIZE - 1
 
@@ -178,13 +188,13 @@
 
 def picks_kernel(slot_ref, landed_hbm, *rest):
     band_hbm = rest[: 3 * BLOCKS]
-    out_hbm, q_ref, piece_ref, acc_ref, lse_ref, out_ref, ins, outs = rest[3 * BLOCKS :]
+    out_hbm, q_ref, piece_ref, acc_ref, sums_ref, out_ref, ins, outs, sums_sems = rest[3 * BLOCKS :]
     rounds = KEY_VALUE_HEADS // PICK_UNROLL
 
     def loads(b, h):
         i = b * KEY_VALUE_HEADS + h
         pairs = [(landed_hbm.at[jnp.maximum(slot_ref[i, p], 0)], piece_ref.at[i, p]) for p in range(PICKED_BLOCKS)]
-        pairs += [(src.at[h], dst.at[i]) for src, dst in zip(band_hbm[3 * b : 3 * b + 3], (q_ref, acc_ref, lse_ref))]
+        pairs += [(src.at[h], dst.at[i]) for src, dst in zip(band_hbm[3 * b : 3 * b + 2], (q_ref, acc_ref))]
         return [pltpu.make_async_copy(src, dst, ins.at[i, n]) for n, (src, dst) in enumerate(pairs)]
 
     def store(b, h):
@@ -198,19 +208,25 @@
             for copy in loads(b, j * PICK_UNROLL + u):
                 copy.start()
 
-    def step(i):
+    def sums_load(b):
+        return pltpu.make_async_copy(band_hbm[3 * b + 2], sums_ref.at[b], sums_sems.at[b])
+
+    def step(b, h):
+        i = b * KEY_VALUE_HEADS + h
         bias = jnp.where(slot_ref[i, 0] >= 0, 0.0, masked_score)
         key = jnp.concatenate([piece_ref[i, p, 0] for p in range(PICKED_BLOCKS)], 0)
+        lane = lax.broadcasted_iota(jnp.int32, key.shape, 1)
+        minus = jnp.where((lane >= PARTS * h) & (lane < PARTS * h + PARTS), -1.0, 0.0).astype(key.dtype)
+        key = jnp.concatenate([key, minus], 1)
         value = jnp.concatenate([piece_ref[i, p, 1] for p in range(PICKED_BLOCKS)], 0)
         for first in range(0, ROWS, PICK_ROWS):
             part = slice(first, first + PICK_ROWS)
-            score = scores_of(q_ref[i, part, :], key)
-            old = lse_ref[i, part, :]
-            best = jnp.broadcast_to(jnp.max(score, -1, keepdims=True) * score_factor, old.shape) + bias
-            top = jnp.maximum(best, old)
+            score = scores_of(jnp.concatenate([q_ref[i, part, :], sums_ref[b, part, :]], 1), key)
+            best = jnp.max(score, -1, keepdims=True) * score_factor + bias
+            top = jnp.maximum(jnp.broadcast_to(best, (PICK_ROWS, HEAD_SIZE)), 0.0)
             shift = top - bias
             weight = jnp.exp2(score * score_factor - jnp.concatenate([shift] * PICKED_BLOCKS, 1))
-            fade = jnp.exp2(old - top)
+            fade = jnp.exp2(-top)
             out, total = summed(weight.astype(jnp.bfloat16), value)
             out = out + acc_ref[i, part, :].astype(jnp.float32) * fade
             result = (out / (total + fade)).astype(out_ref.dtype)
@@ -218,10 +234,14 @@
                 at = slice(g * BLOCK_TOKENS, (g + 1) * BLOCK_TOKENS)
                 out_ref[i, :, first + g * HEAD_SIZE : first + (g + 1) * HEAD_SIZE] = result[at]
 
+    sums_load(0).start()
     for j in range(PICK_AHEAD):
         start_round(0, j)
+    for b in range(1, BLOCKS):
+        sums_load(b).start()
 
     for b in range(BLOCKS):
+        sums_load(b).wait()
 
         @pl.loop(0, rounds)
         def _(j):
@@ -241,7 +261,7 @@
 
             for u in range(PICK_UNROLL):
                 h = j * PICK_UNROLL + u
-                step(b * KEY_VALUE_HEADS + h)
+                step(b, h)
                 store(b, h).start()
 
     for b in range(BLOCKS):
@@ -260,7 +280,8 @@
     smem = pl.BlockSpec(memory_space=SMEM)
     hbm = pl.BlockSpec(memory_space=pl.ANY)
 
-    near_v = lax.ppermute(values, "ctx", [(i - 1, i) for i in range(1, window)])
+    behind = [((i - 1) % window, i) for i in range(window)]
+    near_v = lax.ppermute(values, "ctx", behind)
     rotated_keys, last, table, slot = pl.pallas_call(
         functools.partial(prep_kernel, limit),
         out_shape=(
@@ -275,10 +296,10 @@
         name="prep",
     )(picks.transpose(0, 2, 1), keys, values, cosine, sine)
 
-    near_k = lax.ppermute(rotated_keys, "ctx", [(i - 1, i) for i in range(1, window)])
+    near_k = lax.ppermute(rotated_keys, "ctx", behind)
     wanted = lax.all_to_all(table, "ctx", split_axis=0, concat_axis=0, tiled=True)
-    wanted, last, near_k, near_v = lax.optimization_barrier((wanted, last, near_k, near_v))
-    far_even = lax.ppermute(last, "ctx", [(i - 2, i) for i in range(2, window, 2)])
+    wanted, near_k, near_v = lax.optimization_barrier((wanted, near_k, near_v))
+    far_even = lax.ppermute(last, "ctx", [((i - 2 if i % 2 == 0 else i + 2) % window, i) for i in range(window)])
 
     answer = pl.pallas_call(
         gather_kernel,
@@ -301,7 +322,7 @@
             out_shape=(
                 jax.ShapeDtypeStruct(full, bf16),
                 jax.ShapeDtypeStruct(full, bf16),
-                jax.ShapeDtypeStruct(full, jnp.float32),
+                jax.ShapeDtypeStruct((ROWS, HEAD_SIZE), bf16),
             ),
             in_specs=[smem] + [vmem] * (7 + len(far)),
             out_specs=(vmem,) * 3,
@@ -313,7 +334,7 @@
     second = band(1, 50)
     edge_k, edge_v, _ = lax.optimization_barrier((near_k, near_v, second[2]))
     edge = jnp.concatenate([edge_k[tokens - BLOCK_TOKENS :], edge_v[tokens - BLOCK_TOKENS :]], 1)
-    far_odd = lax.ppermute(edge, "ctx", [(i - 1, i) for i in range(1, window, 2)])
+    far_odd = lax.ppermute(edge, "ctx", [(i ^ 1, i) for i in range(window)])
     first = band(0, 1, far_even, far_odd)
 
     count = BLOCKS * KEY_VALUE_HEADS
@@ -327,10 +348,11 @@
             pltpu.VMEM(narrow, bf16),
             pltpu.VMEM((count, PICKED_BLOCKS, 2, BLOCK_TOKENS, HEAD_SIZE), bf16),
             pltpu.VMEM(narrow, bf16),
-            pltpu.VMEM(narrow, jnp.float32),
+            pltpu.VMEM((BLOCKS, ROWS, HEAD_SIZE), bf16),
             pltpu.VMEM((count, BLOCK_TOKENS, ROWS), bf16),
-            pltpu.SemaphoreType.DMA((count, PICKED_BLOCKS + 3)),
+            pltpu.SemaphoreType.DMA((count, PICKED_BLOCKS + 2)),
             pltpu.SemaphoreType.DMA((count,)),
+            pltpu.SemaphoreType.DMA((BLOCKS,)),
         ],
         cost_estimate=pl.CostEstimate(flops=2 * band_flops, bytes_accessed=16 << 20, transcendentals=1 << 22),
         compiler_params=pltpu.CompilerParams(vmem_limit_bytes=58 << 20),

time: 94.5 us -> 88.1 us (0.932)
  starting transfers between devices: 22.6 us -> 14.9 us
  Pallas kernels: 38.8 us -> 40.1 us
  waiting for transfers between devices: 20.1 us -> 21.4 us
  local copies, waits for them, and re-layouts: 10.2 us -> 9.09 us
    ppermute x4, starting transfers between devices: 8.42 us -> 2.6 us  [the longest x1 1.83 us: shards(): near_v = lax.ppermute(values, 'ctx', behind)]
    all_to_all x1, waiting for transfers between devices: 13.9 us -> 17.1 us  [shards(): lax.all_to_all(answer, 'ctx', split_axis=0, concat_axis=0, tiled=True)]
    all_to_all x1, starting transfers between devices: 8.8 us -> 6.88 us  [shards(): lax.all_to_all(answer, 'ctx', split_axis=0, concat_axis=0, tiled=True)]
    ppermute x4, waiting for transfers between devices: 2.49 us -> 0.74 us  [the longest x1 0.73 us: shards(): far_odd = lax.ppermute(edge, 'ctx', [(i ^ 1, i) for i in range(window)])]
    pallas_call x2, Pallas kernels: 19.5 us -> 20.7 us  [band(): pl.pallas_call(functools.partial(band_kernel, b), out_shape=(jax.ShapeDty...]
    unnamed x24, local copies, waits for them, and re-layouts: 10.1 us -> 9.05 us
  transfers between devices with their start and end apart: 6 -> 6, of which waited for: 3 -> 3; matrix products, arithmetic and copies ran while one was open for 2% -> 2% of each run, Pallas kernels for 28% -> 31%
where the time goes in v3:
time: 88.1 us; the launch traced here: 87.7 us
  Pallas kernels  40.1 us (46%)
  waiting for transfers between devices  21.4 us (24%)
  starting transfers between devices  14.9 us (17%)
  local copies, waits for them, and re-layouts  9.09 us (10%)
  other arithmetic  2.06 us (2%)
    pallas_call x2, Pallas kernels, band(): pl.pallas_call(functools.partial(band_kernel, b), out_shape=(jax.ShapeDty...  20.7 us
    all_to_all x1, waiting for transfers between devices, shards(): lax.all_to_all(answer, 'ctx', split_axis=0, concat_axis=0, tiled=True)  17.1 us
    pallas_call x1, Pallas kernels, shards(): pl.pallas_call(picks_kernel, out_shape=jax.ShapeDtypeStruct((tokens, QUER...  13 us
    unnamed x24, local copies, waits for them, and re-layouts  9.05 us
    all_to_all x1, starting transfers between devices, shards(): lax.all_to_all(answer, 'ctx', split_axis=0, concat_axis=0, tiled=True)  6.88 us
    all_to_all x1, starting transfers between devices, shards(): lax.all_to_all(table, 'ctx', split_axis=0, concat_axis=0, tiled=True)  5.39 us
    all_to_all x1, waiting for transfers between devices, shards(): lax.all_to_all(table, 'ctx', split_axis=0, concat_axis=0, tiled=True)  3.61 us
    pallas_call x1, Pallas kernels, shards(): pl.pallas_call(functools.partial(prep_kernel, limit), out_shape=(jax.Shap...  3.28 us
  transfers between devices with their start and end apart: 6, of which 3 were waited for; matrix products, arithmetic and copies ran while one was open for 2% of the time, Pallas kernels for 31%

profile of v3, /device:TPU:15, one launch (start us, length us, event | category | flops | bytes accessed | tf_op | source)
XLA Modules:
  0.0 87.7 jit_solution(9749778215543901917)
XLA Ops:
  0.0 1.8 %collective-permute-start.1 = (bf16[256,1024]{1,0:T(8,128)(2,1)}, bf16[256,1024]{1,0:T(8,128)(2,1)S(1)}, u32[]{:S(2)}, u32[]{:S(2)}) collective-permute-start(bf16[256,1024]{1,0:T(8,128)(2,1)} %v_ref.7), channel_id=1, source_target_pairs={{15,0},{0,1},{1,2},{2,3},{3,4},{4,5},{5,6},{6,7},{7,8},{8,9},{9,10... | collective-permute-start | bytes 1572872 | tf_op jit(solution)/shard_map/ppermute | solution.py:284
  1.8 0.1 compare_select_fusion
  1.9 0.7 convert_element_type.3
  2.6 1.3 %fusion = (f32[256,128]{1,0:T(8,128)}, f32[256,128]{1,0:T(8,128)}) fusion(f32[128]{0:T(128)S(1)} %get-tuple-element.37, f32[128]{0:T(128)S(1)} %get-tuple-element.38, f32[256]{0:T(256)S(1)} %convert_element_type.3), kind=kLoop, calls=%fused_computation.3 | loop fusion | flops 65536 | bytes 264192 | tf_op jit(solution)/shard_map/mul | solution.py:41
  3.9 3.3 %prep.1 = (bf16[256,1024]{1,0:T(8,128)(2,1)}, bf16[128,2048]{1,0:T(8,128)(2,1)}, s32[16,1,2]{2,1,0:T(1,128)}, s32[16,2]{1,0:T(8,128)}) custom-call(s32[2,2,8]{2,1,0:T(2,128)} %bitcast.3, bf16[256,1024]{1,0:T(8,128)(2,1)} %k_ref.1, bf16[256,1024]{1,0:T(8,128)(2,1)} %v_ref.7, f32[256,128]{1,0:T(8,128)} %get-tuple-element.36.cos_ref, ...), custom_call_target="tpu_custom_call" | custom-call | tf_op jit(solution)/shard_map/prep/pallas_call | solution.py:285
  7.2 0.1 collective-permute-start
  7.2 5.4 %all-to-all-start = ((s32[16,1,2]{2,1,0:T(1,128)}), s32[16,1,2]{2,1,0:T(1,128)S(1)}, u32[]{:S(2)}, u32[]{:S(2)}) async-start(s32[16,1,2]{2,1,0:T(1,128)} %get-tuple-element.21), calls=%async_computation | async-start | bytes 16384 | tf_op jit(solution)/shard_map/all_to_all | solution.py:300
  12.6 0.3 collective-permute-start.2
  12.9 3.6 %all-to-all-done.wanted_ref = s32[16,1,2]{2,1,0:T(1,128)S(1)} async-done(((s32[16,1,2]{2,1,0:T(1,128)}), s32[16,1,2]{2,1,0:T(1,128)S(1)}, u32[]{:S(2)}, u32[]{:S(2)}) %all-to-all-start) | async-done | bytes 160 | tf_op jit(solution)/shard_map/all_to_all | solution.py:300
  16.5 0.0 copy-start.11
  16.5 0.0 collective-permute-done.1.nv_ref
  16.5 0.0 collective-permute-done.nk_ref
  16.5 0.6 copy-done.11
  17.1 3.1 %gather.1 = bf16[16,2,2,128,128]{4,3,2,1,0:T(8,128)(2,1)} custom-call(s32[16,1,2]{2,1,0:T(1,128)} %copy-done.11, bf16[256,1024]{1,0:T(8,128)(2,1)} %get-tuple-element.22.k_ref, bf16[256,1024]{1,0:T(8,128)(2,1)} %v_ref.7), custom_call_target="tpu_custom_call" | custom-call | bytes 62914560 | tf_op jit(solution)/shard_map/gather/pallas_call | solution.py:304
  20.2 0.0 copy-start
  20.2 0.0 copy-start.1
  20.2 0.0 copy-start.2
  20.2 0.0 copy-start.3
  20.2 6.9 %all-to-all-start.1 = ((bf16[16,2,2,128,128]{4,3,2,1,0:T(8,128)(2,1)}), bf16[16,2,2,128,128]{4,3,2,1,0:T(8,128)(2,1)}, u32[]{:S(2)}, u32[]{:S(2)}) async-start(bf16[16,2,2,128,128]{4,3,2,1,0:T(8,128)(2,1)} %gather.1), calls=%async_computation.1 | async-start | bytes 4194304 | tf_op jit(solution)/shard_map/all_to_all | solution.py:313
  27.1 0.0 copy-done
  27.1 0.0 copy-done.1
  27.1 0.0 copy-done.2
  27.1 0.0 copy-done.3
  27.1 0.0 copy-start.4
  27.1 2.2 %copy-done.4 = bf16[256,8192]{1,0:T(8,128)(2,1)S(1)} copy-done((bf16[256,8192]{1,0:T(8,128)(2,1)S(1)}, bf16[256,8192]{1,0:T(8,128)(2,1)}, u32[]{:S(2)}) %copy-start.4) | copy-done | bytes 4194328
  29.3 9.8 %band.2 = (bf16[8,1024,128]{2,1,0:T(8,128)(2,1)S(1)}, bf16[8,1024,128]{2,1,0:T(8,128)(2,1)S(1)}, bf16[1024,128]{1,0:T(8,128)(2,1)S(1)}) custom-call(s32[1]{0:T(128)} %bitcast.2.me_ref, bf16[256,8192]{1,0:T(8,128)(2,1)S(1)} %copy-done.4, f32[256,128]{1,0:T(8,128)S(1)} %copy-done.2, f32[256,128]{1,0:T(8,128)S(1)} %copy-done.1, ...), custom_call_target="tpu_custom_call" | custom-call | flops 214748364800 | bytes 8388608 | tf_op jit(solution)/shard_map/band/pallas_call | solution.py:320
  39.2 0.0 copy-start.7
  39.2 1.3 %copy-done.7 = bf16[8,1024,128]{2,1,0:T(8,128)(2,1)} copy-done((bf16[8,1024,128]{2,1,0:T(8,128)(2,1)}, bf16[8,1024,128]{2,1,0:T(8,128)(2,1)S(1)}, u32[]{:S(2)}) %copy-start.7) | copy-done | bytes 2097176
  40.5 0.0 copy-start.10
  40.5 0.7 copy-done.10
  41.2 0.0 copy-start.8
  41.3 0.4 collective-permute-start.3
  41.7 0.0 collective-permute-done.2.rest_0_
  41.7 0.8 copy-done.8
  42.5 0.7 collective-permute-done.3.rest_1_
  43.2 10.8 %band.3 = (bf16[8,1024,128]{2,1,0:T(8,128)(2,1)S(1)}, bf16[8,1024,128]{2,1,0:T(8,128)(2,1)S(1)}, bf16[1024,128]{1,0:T(8,128)(2,1)S(1)}) custom-call(s32[1]{0:T(128)} %bitcast.2.me_ref, bf16[256,8192]{1,0:T(8,128)(2,1)S(1)} %copy-done.4, f32[256,128]{1,0:T(8,128)S(1)} %copy-done.2, f32[256,128]{1,0:T(8,128)S(1)} %copy-done.1, ...), custom_call_target="tpu_custom_call" | custom-call | flops 4294967296 | bytes 8388608 | tf_op jit(solution)/shard_map/band/pallas_call | solution.py:320
  54.1 0.0 copy-start.5
  54.1 1.4 %copy-done.5 = bf16[8,1024,128]{2,1,0:T(8,128)(2,1)} copy-done((bf16[8,1024,128]{2,1,0:T(8,128)(2,1)}, bf16[8,1024,128]{2,1,0:T(8,128)(2,1)S(1)}, u32[]{:S(2)}) %copy-start.5) | copy-done | bytes 2097176
  55.5 0.0 copy-start.6
  55.5 1.4 %copy-done.6 = bf16[8,1024,128]{2,1,0:T(8,128)(2,1)} copy-done((bf16[8,1024,128]{2,1,0:T(8,128)(2,1)}, bf16[8,1024,128]{2,1,0:T(8,128)(2,1)S(1)}, u32[]{:S(2)}) %copy-start.6) | copy-done | bytes 2097176
  56.8 0.0 copy-start.9
  56.8 0.7 copy-done.9
  57.5 17.1 %all-to-all-done.1 = bf16[16,2,2,128,128]{4,3,2,1,0:T(8,128)(2,1)} async-done(((bf16[16,2,2,128,128]{4,3,2,1,0:T(8,128)(2,1)}), bf16[16,2,2,128,128]{4,3,2,1,0:T(8,128)(2,1)}, u32[]{:S(2)}, u32[]{:S(2)}) %all-to-all-start.1) | async-done | bytes 2097184 | tf_op jit(solution)/shard_map/all_to_all | solution.py:313
  74.6 13.0 %picks.1 = bf16[256,8192]{1,0:T(8,128)(2,1)} custom-call(s32[16,2]{1,0:T(8,128)} %get-tuple-element.20.slot_ref, bf16[32,2,128,128]{3,2,1,0:T(8,128)(2,1)} %bitcast.1.landed_hbm, bf16[8,1024,128]{2,1,0:T(8,128)(2,1)} %copy-done.5, bf16[8,1024,128]{2,1,0:T(8,128)(2,1)} %copy-done.6, bf16[1024,128]{1,0:T(8,128)(2,1)} %copy-done.9, ...), custom_call_target="tpu_custom_call" | custom-call | flops 8589934592 | bytes 16777216 | tf_op jit(solution)/shard_map/picks/pallas_call | solution.py:342
  (4 shorter events, 0.1 us)
Async XLA Ops:
  0.0 16.5 %collective-permute-start.1 = (bf16[256,1024]{1,0:T(8,128)(2,1)}, bf16[256,1024]{1,0:T(8,128)(2,1)S(1)}, u32[]{:S(2)}, u32[]{:S(2)}) collective-permute-start(bf16[256,1024]{1,0:T(8,128)(2,1)} %v_ref.7), channel_id=1, source_target_pairs={{15,0},{0,1},{1,2},{2,3},{3,4},{4,5},{5,6},{6,7},{7,8},{8,9},{9,10... | collective-permute-start | bytes 1572872 | tf_op jit(solution)/shard_map/ppermute | solution.py:284
  7.2 9.4 %collective-permute-start = (bf16[256,1024]{1,0:T(8,128)(2,1)}, bf16[256,1024]{1,0:T(8,128)(2,1)S(1)}, u32[]{:S(2)}, u32[]{:S(2)}) collective-permute-start(bf16[256,1024]{1,0:T(8,128)(2,1)} %get-tuple-element.22.k_ref), channel_id=1, source_target_pairs={{15,0},{0,1},{1,2},{2,3},{3,4},{4,5},{5,6},{6,7},{7,8},{8,9},{9,10... | collective-permute-start | bytes 1572872 | tf_op jit(solution)/shard_map/ppermute | solution.py:299
  7.2 9.3 %all-to-all-start = ((s32[16,1,2]{2,1,0:T(1,128)}), s32[16,1,2]{2,1,0:T(1,128)S(1)}, u32[]{:S(2)}, u32[]{:S(2)}) async-start(s32[16,1,2]{2,1,0:T(1,128)} %get-tuple-element.21), calls=%async_computation | async-start | bytes 16384 | tf_op jit(solution)/shard_map/all_to_all | solution.py:300
  12.6 29.1 %collective-permute-start.2 = (bf16[128,2048]{1,0:T(8,128)(2,1)}, bf16[128,2048]{1,0:T(8,128)(2,1)}, u32[]{:S(2)}, u32[]{:S(2)}) collective-permute-start(bf16[128,2048]{1,0:T(8,128)(2,1)} %get-tuple-element.26), channel_id=1, source_target_pairs={{14,0},{3,1},{0,2},{5,3},{2,4},{7,5},{4,6},{9,7},{6,8},{11,9},{8,1... | collective-permute-start | bytes 1572872 | tf_op jit(solution)/shard_map/ppermute | solution.py:302
  16.5 0.6 copy-start.11
  20.2 6.9 %copy-start = (bf16[256,1024]{1,0:T(8,128)(2,1)S(1)}, bf16[256,1024]{1,0:T(8,128)(2,1)}, u32[]{:S(2)}) copy-start(bf16[256,1024]{1,0:T(8,128)(2,1)} %v_ref.7) | copy-start | bytes 1572868
  20.2 6.9 %copy-start.1 = (f32[256,128]{1,0:T(8,128)S(1)}, f32[256,128]{1,0:T(8,128)}, u32[]{:S(2)}) copy-start(f32[256,128]{1,0:T(8,128)} %get-tuple-element.35.sin_ref) | copy-start | bytes 393220
  20.2 6.9 %copy-start.2 = (f32[256,128]{1,0:T(8,128)S(1)}, f32[256,128]{1,0:T(8,128)}, u32[]{:S(2)}) copy-start(f32[256,128]{1,0:T(8,128)} %get-tuple-element.36.cos_ref) | copy-start | bytes 393220
  20.2 6.9 %copy-start.3 = (bf16[256,1024]{1,0:T(8,128)(2,1)S(1)}, bf16[256,1024]{1,0:T(8,128)(2,1)}, u32[]{:S(2)}) copy-start(bf16[256,1024]{1,0:T(8,128)(2,1)} %get-tuple-element.22.k_ref) | copy-start | bytes 1572868
  20.2 54.4 %all-to-all-start.1 = ((bf16[16,2,2,128,128]{4,3,2,1,0:T(8,128)(2,1)}), bf16[16,2,2,128,128]{4,3,2,1,0:T(8,128)(2,1)}, u32[]{:S(2)}, u32[]{:S(2)}) async-start(bf16[16,2,2,128,128]{4,3,2,1,0:T(8,128)(2,1)} %gather.1), calls=%async_computation.1 | async-start | bytes 4194304 | tf_op jit(solution)/shard_map/all_to_all | solution.py:313
  27.1 2.2 %copy-start.4 = (bf16[256,8192]{1,0:T(8,128)(2,1)S(1)}, bf16[256,8192]{1,0:T(8,128)(2,1)}, u32[]{:S(2)}) copy-start(bf16[256,8192]{1,0:T(8,128)(2,1)} %q_ref.3) | copy-start | bytes 12582916
  39.2 1.3 %copy-start.7 = (bf16[8,1024,128]{2,1,0:T(8,128)(2,1)}, bf16[8,1024,128]{2,1,0:T(8,128)(2,1)S(1)}, u32[]{:S(2)}) copy-start(bf16[8,1024,128]{2,1,0:T(8,128)(2,1)S(1)} %get-tuple-element.33.rest_3_) | copy-start | bytes 6291460
  40.5 0.7 copy-start.10
  41.2 1.3 %copy-start.8 = (bf16[8,1024,128]{2,1,0:T(8,128)(2,1)}, bf16[8,1024,128]{2,1,0:T(8,128)(2,1)S(1)}, u32[]{:S(2)}) copy-start(bf16[8,1024,128]{2,1,0:T(8,128)(2,1)S(1)} %get-tuple-element.34.rest_4_) | copy-start | bytes 6291460
  41.3 2.0 %collective-permute-start.3 = (bf16[128,2048]{1,0:T(8,128)(2,1)S(1)}, bf16[128,2048]{1,0:T(8,128)(2,1)S(1)}, u32[]{:S(2)}, u32[]{:S(2)}) collective-permute-start(bf16[128,2048]{1,0:T(8,128)(2,1)S(1)} %pad_maximum_fusion), channel_id=1, source_target_pairs={{1,0},{0,1},{3,2},{2,3},{5,4},{4,5},{7,6},{6,7},{9,8},{8,9},{11,10... | collective-permute-start | bytes 1572872 | tf_op jit(solution)/shard_map/ppermute | solution.py:337
  54.1 1.4 %copy-start.5 = (bf16[8,1024,128]{2,1,0:T(8,128)(2,1)}, bf16[8,1024,128]{2,1,0:T(8,128)(2,1)S(1)}, u32[]{:S(2)}) copy-start(bf16[8,1024,128]{2,1,0:T(8,128)(2,1)S(1)} %get-tuple-element.30.rest_0_) | copy-start | bytes 6291460
  55.5 1.4 %copy-start.6 = (bf16[8,1024,128]{2,1,0:T(8,128)(2,1)}, bf16[8,1024,128]{2,1,0:T(8,128)(2,1)S(1)}, u32[]{:S(2)}) copy-start(bf16[8,1024,128]{2,1,0:T(8,128)(2,1)S(1)} %get-tuple-element.31.rest_1_) | copy-start | bytes 6291460
  56.8 0.7 copy-start.9

commit v4 on v3

--- a/solution.py
+++ b/solution.py
@@ -2,6 +2,7 @@
 
 import jax
 import jax.numpy as jnp
+import numpy as np
 from jax import lax
 from jax.experimental import pallas as pl
 from jax.experimental.pallas import tpu as pltpu
@@ -27,18 +28,16 @@
 
 BAND_ROWS = 256
 PICK_ROWS = 512
-PICK_UNROLL = 4
-PICK_AHEAD = 2
+PICK_UNROLL = 8
+PICK_AHEAD = 1
 
 SMEM = pltpu.MemorySpace.SMEM
 
 
-def rotary_tables(pos):
+def frequencies():
     half = HEAD_SIZE // 2
-    freq = rope_base ** (-(jnp.arange(half, dtype=jnp.float32) * 2.0) / HEAD_SIZE)
-    angle = pos.astype(jnp.float32)[:, None] * jnp.concatenate([freq, freq])[None, :]
-    sign = jnp.where(jnp.arange(HEAD_SIZE) < half, -1.0, 1.0)
-    return jnp.cos(angle), jnp.sin(angle) * sign[None, :]
+    freq = rope_base ** (-(np.arange(half, dtype=np.float64) * 2.0) / HEAD_SIZE)
+    return np.concatenate([freq, freq])[None, :].astype(np.float32)
 
 
 def rotate(x, cosine, sine):
@@ -47,7 +46,9 @@
     return (wide * cosine + swapped * sine).astype(jnp.bfloat16)
 
 
-def prep_kernel(limit, picks_ref, k_ref, v_ref, cos_ref, sin_ref, kr_ref, last_ref, table_ref, slot_ref, count_ref):
+def prep_kernel(
+    limit, picks_ref, k_ref, v_ref, pos_ref, freq_ref, kr_ref, last_ref, cos_ref, sin_ref, table_ref, slot_ref, count_ref
+):
     shards = table_ref.shape[0]
 
     @pl.loop(0, shards)
@@ -72,10 +73,20 @@
                 table_ref[owner, 0, rank] = pick % BLOCKS * KEY_VALUE_HEADS + h
                 slot_ref[i, p] = owner * limit + rank
 
+    spread = [
+        jnp.broadcast_to(pos_ref[b : b + 1, :].astype(jnp.float32), (BLOCK_TOKENS, BLOCK_TOKENS)).T
+        for b in range(BLOCKS)
+    ]
+    upper = lax.broadcasted_iota(jnp.int32, spread[0].shape, 1) >= HEAD_SIZE // 2
+    angle = jnp.where(upper, spread[1], spread[0]) * freq_ref[...]
+    cosines = jnp.cos(angle)
+    sines = jnp.sin(angle)
     for b in range(BLOCKS):
         rows = slice(b * BLOCK_TOKENS, (b + 1) * BLOCK_TOKENS)
-        cosine = cos_ref[rows, :]
-        sine = sin_ref[rows, :]
+        cosine, sine = (jnp.where(upper == (b == 1), x, pltpu.roll(x, HEAD_SIZE // 2, 1)) for x in (cosines, sines))
+        sine = jnp.where(upper, sine, -sine)
+        cos_ref[rows, :] = cosine
+        sin_ref[rows, :] = sine
         for h in range(KEY_VALUE_HEADS):
             cols = slice(h * HEAD_SIZE, (h + 1) * HEAD_SIZE)
             rotated = rotate(k_ref[rows, cols], cosine, sine)
@@ -274,7 +285,6 @@
     window = lax.axis_size("ctx")
     limit = max(1, BLOCKS * KEY_VALUE_HEADS * PICKED_BLOCKS // window)
     me = lax.axis_index("ctx").astype(jnp.int32).reshape(1)
-    cosine, sine = rotary_tables(positions)
     bf16 = jnp.bfloat16
     vmem = pl.BlockSpec(memory_space=pltpu.MemorySpace.VMEM)
     smem = pl.BlockSpec(memory_space=SMEM)
@@ -282,24 +292,26 @@
 
     behind = [((i - 1) % window, i) for i in range(window)]
     near_v = lax.ppermute(values, "ctx", behind)
-    rotated_keys, last, table, slot = pl.pallas_call(
+    rotated_keys, last, cosine, sine, table, slot = pl.pallas_call(
         functools.partial(prep_kernel, limit),
         out_shape=(
             jax.ShapeDtypeStruct((tokens, KEY_WIDTH), bf16),
             jax.ShapeDtypeStruct((BLOCK_TOKENS, 2 * KEY_WIDTH), bf16),
+            jax.ShapeDtypeStruct((tokens, HEAD_SIZE), jnp.float32),
+            jax.ShapeDtypeStruct((tokens, HEAD_SIZE), jnp.float32),
             jax.ShapeDtypeStruct((window, 1, limit), jnp.int32),
             jax.ShapeDtypeStruct((BLOCKS * KEY_VALUE_HEADS, PICKED_BLOCKS), jnp.int32),
         ),
         in_specs=[smem, vmem, vmem, vmem, vmem],
-        out_specs=(vmem, vmem, smem, smem),
+        out_specs=(vmem, vmem, vmem, vmem, smem, smem),
         scratch_shapes=[pltpu.SMEM((window,), jnp.int32)],
         name="prep",
-    )(picks.transpose(0, 2, 1), keys, values, cosine, sine)
+    )(picks.transpose(0, 2, 1), keys, values, positions.reshape(BLOCKS, BLOCK_TOKENS), jnp.asarray(frequencies()))
 
     near_k = lax.ppermute(rotated_keys, "ctx", behind)
     wanted = lax.all_to_all(table, "ctx", split_axis=0, concat_axis=0, tiled=True)
     wanted, near_k, near_v = lax.optimization_barrier((wanted, near_k, near_v))
-    far_even = lax.ppermute(last, "ctx", [((i - 2 if i % 2 == 0 else i + 2) % window, i) for i in range(window)])
+    far_even = lax.ppermute(last, "ctx", [((i - 2) % window, i) for i in range(0, window, 2)])
 
     answer = pl.pallas_call(
         gather_kernel,

time: 88.1 us -> 87.1 us (0.989)
  other arithmetic: 2.06 us -> 0.04 us
  starting transfers between devices: 14.9 us -> 16.3 us
    mul x1 -> x0, other arithmetic: 1.25 us -> none  [rotary_tables(): return (jnp.cos(angle), jnp.sin(angle) * sign[None, :])]
    ppermute x1, starting transfers between devices: 0.28 us -> 1.45 us  [shards(): lax.ppermute(last, 'ctx', [((i - 2) % window, i) for i in range(0, window...]
  transfers between devices with their start and end apart: 6 -> 6, of which waited for: 3 -> 3; matrix products, arithmetic and copies ran while one was open for 2% -> 0% of each run, Pallas kernels for 31% -> 32%
where the time goes in v4:
time: 87.1 us; the launch traced here: 86.7 us
  Pallas kernels  40.3 us (46%)
  waiting for transfers between devices  20.6 us (24%)
  starting transfers between devices  16.3 us (19%)
  local copies, waits for them, and re-layouts  9.12 us (10%)
    pallas_call x2, Pallas kernels, band(): pl.pallas_call(functools.partial(band_kernel, b), out_shape=(jax.ShapeDty...  20.9 us
    all_to_all x1, waiting for transfers between devices, shards(): lax.all_to_all(answer, 'ctx', split_axis=0, concat_axis=0, tiled=True)  16.8 us
    pallas_call x1, Pallas kernels, shards(): pl.pallas_call(picks_kernel, out_shape=jax.ShapeDtypeStruct((tokens, QUER...  12.8 us
    unnamed x24, local copies, waits for them, and re-layouts  9.08 us
    all_to_all x1, starting transfers between devices, shards(): lax.all_to_all(answer, 'ctx', split_axis=0, concat_axis=0, tiled=True)  7.12 us
    all_to_all x1, starting transfers between devices, shards(): lax.all_to_all(table, 'ctx', split_axis=0, concat_axis=0, tiled=True)  5.39 us
    pallas_call x1, Pallas kernels, shards(): pl.pallas_call(functools.partial(prep_kernel, limit), out_shape=(jax.Shap...  3.59 us
    pallas_call x1, Pallas kernels, shards(): pl.pallas_call(gather_kernel, out_shape=jax.ShapeDtypeStruct((window, lim...  3.07 us
  transfers between devices with their start and end apart: 6, of which 3 were waited for; matrix products, arithmetic and copies ran while one was open for 0% of the time, Pallas kernels for 32%

profile of v4, /device:TPU:15, one launch (start us, length us, event | category | flops | bytes accessed | tf_op | source)
XLA Modules:
  0.0 86.7 jit_solution(9018978416678570715)
XLA Ops:
  0.0 1.8 %collective-permute-start.1 = (bf16[256,1024]{1,0:T(8,128)(2,1)}, bf16[256,1024]{1,0:T(8,128)(2,1)S(1)}, u32[]{:S(2)}, u32[]{:S(2)}) collective-permute-start(bf16[256,1024]{1,0:T(8,128)(2,1)} %v_ref.7), channel_id=1, source_target_pairs={{15,0},{0,1},{1,2},{2,3},{3,4},{4,5},{5,6},{6,7},{7,8},{8,9},{9,10... | collective-permute-start | bytes 1572872 | tf_op jit(solution)/shard_map/ppermute | solution.py:294
  1.8 3.6 %prep.1 = (bf16[256,1024]{1,0:T(8,128)(2,1)}, bf16[128,2048]{1,0:T(8,128)(2,1)}, f32[256,128]{1,0:T(8,128)}, f32[256,128]{1,0:T(8,128)}, s32[16,1,2]{2,1,0:T(1,128)}, /*index=5*/s32[16,2]{1,0:T(8,128)}) custom-call(s32[2,2,8]{2,1,0:T(2,128)} %bitcast.4, bf16[256,1024]{1,0:T(8,128)(2,1)} %k_ref.1, bf16[256,1024]{1,0:T(8,128)(2,1)} %v_ref.7, ...), custom_call_target="tpu_custom_call" | custom-call | tf_op jit(solution)/shard_map/prep/pallas_call | solution.py:295
  5.4 0.1 collective-permute-start
  5.5 5.4 %all-to-all-start = ((s32[16,1,2]{2,1,0:T(1,128)}), s32[16,1,2]{2,1,0:T(1,128)S(1)}, u32[]{:S(2)}, u32[]{:S(2)}) async-start(s32[16,1,2]{2,1,0:T(1,128)} %get-tuple-element.23), calls=%async_computation | async-start | bytes 16384 | tf_op jit(solution)/shard_map/all_to_all | solution.py:312
  10.9 1.5 %collective-permute-start.2 = (bf16[128,2048]{1,0:T(8,128)(2,1)}, bf16[128,2048]{1,0:T(8,128)(2,1)}, u32[]{:S(2)}, u32[]{:S(2)}) collective-permute-start(bf16[128,2048]{1,0:T(8,128)(2,1)} %get-tuple-element.30), channel_id=1, source_target_pairs={{14,0},{0,2},{2,4},{4,6},{6,8},{8,10},{10,12},{12,14},{30,16},{16,... | collective-permute-start | bytes 1572872 | tf_op jit(solution)/shard_map/ppermute | solution.py:314
  12.3 3.0 %all-to-all-done.wanted_ref = s32[16,1,2]{2,1,0:T(1,128)S(1)} async-done(((s32[16,1,2]{2,1,0:T(1,128)}), s32[16,1,2]{2,1,0:T(1,128)S(1)}, u32[]{:S(2)}, u32[]{:S(2)}) %all-to-all-start) | async-done | bytes 160 | tf_op jit(solution)/shard_map/all_to_all | solution.py:312
  15.3 0.0 copy-start.11
  15.3 0.0 collective-permute-done.1.nv_ref
  15.3 0.0 collective-permute-done.nk_ref
  15.3 0.6 copy-done.11
  15.9 3.1 %gather.1 = bf16[16,2,2,128,128]{4,3,2,1,0:T(8,128)(2,1)} custom-call(s32[16,1,2]{2,1,0:T(1,128)} %copy-done.11, bf16[256,1024]{1,0:T(8,128)(2,1)} %get-tuple-element.24.k_ref, bf16[256,1024]{1,0:T(8,128)(2,1)} %v_ref.7), custom_call_target="tpu_custom_call" | custom-call | bytes 62914560 | tf_op jit(solution)/shard_map/gather/pallas_call | solution.py:316
  19.0 0.0 copy-start
  19.0 0.0 copy-start.1
  19.0 0.0 copy-start.3
  19.0 0.0 copy-start.4
  19.0 7.1 %all-to-all-start.1 = ((bf16[16,2,2,128,128]{4,3,2,1,0:T(8,128)(2,1)}), bf16[16,2,2,128,128]{4,3,2,1,0:T(8,128)(2,1)}, u32[]{:S(2)}, u32[]{:S(2)}) async-start(bf16[16,2,2,128,128]{4,3,2,1,0:T(8,128)(2,1)} %gather.1), calls=%async_computation.1 | async-start | bytes 4194304 | tf_op jit(solution)/shard_map/all_to_all | solution.py:325
  26.1 0.0 copy-done
  26.1 0.0 copy-done.1
  26.2 0.0 copy-done.3
  26.2 0.0 copy-done.4
  26.2 0.0 copy-start.2
  26.2 2.2 %copy-done.2 = bf16[256,8192]{1,0:T(8,128)(2,1)S(1)} copy-done((bf16[256,8192]{1,0:T(8,128)(2,1)S(1)}, bf16[256,8192]{1,0:T(8,128)(2,1)}, u32[]{:S(2)}) %copy-start.2) | copy-done | bytes 4194328
  28.4 9.8 %band.2 = (bf16[8,1024,128]{2,1,0:T(8,128)(2,1)S(1)}, bf16[8,1024,128]{2,1,0:T(8,128)(2,1)S(1)}, bf16[1024,128]{1,0:T(8,128)(2,1)S(1)}) custom-call(s32[1]{0:T(128)} %bitcast.3.me_ref, bf16[256,8192]{1,0:T(8,128)(2,1)S(1)} %copy-done.2, f32[256,128]{1,0:T(8,128)S(1)} %copy-done.3, f32[256,128]{1,0:T(8,128)S(1)} %copy-done.4, ...), custom_call_target="tpu_custom_call" | custom-call | flops 214748364800 | bytes 8388608 | tf_op jit(solution)/shard_map/band/pallas_call | solution.py:332
  38.2 0.0 copy-start.8
  38.2 1.3 %copy-done.8 = bf16[8,1024,128]{2,1,0:T(8,128)(2,1)} copy-done((bf16[8,1024,128]{2,1,0:T(8,128)(2,1)}, bf16[8,1024,128]{2,1,0:T(8,128)(2,1)S(1)}, u32[]{:S(2)}) %copy-start.8) | copy-done | bytes 2097176
  39.6 0.0 copy-start.10
  39.6 0.7 copy-done.10
  40.3 0.0 copy-start.7
  40.4 0.4 collective-permute-start.3
  40.8 0.0 collective-permute-done.2.rest_0_
  40.8 0.8 copy-done.7
  41.6 0.8 collective-permute-done.3.rest_1_
  42.3 11.0 %band.3 = (bf16[8,1024,128]{2,1,0:T(8,128)(2,1)S(1)}, bf16[8,1024,128]{2,1,0:T(8,128)(2,1)S(1)}, bf16[1024,128]{1,0:T(8,128)(2,1)S(1)}) custom-call(s32[1]{0:T(128)} %bitcast.3.me_ref, bf16[256,8192]{1,0:T(8,128)(2,1)S(1)} %copy-done.2, f32[256,128]{1,0:T(8,128)S(1)} %copy-done.3, f32[256,128]{1,0:T(8,128)S(1)} %copy-done.4, ...), custom_call_target="tpu_custom_call" | custom-call | flops 4294967296 | bytes 8388608 | tf_op jit(solution)/shard_map/band/pallas_call | solution.py:332
  53.4 0.0 copy-start.5
  53.4 1.4 %copy-done.5 = bf16[8,1024,128]{2,1,0:T(8,128)(2,1)} copy-done((bf16[8,1024,128]{2,1,0:T(8,128)(2,1)}, bf16[8,1024,128]{2,1,0:T(8,128)(2,1)S(1)}, u32[]{:S(2)}) %copy-start.5) | copy-done | bytes 2097176
  54.7 0.0 copy-start.6
  54.7 1.4 %copy-done.6 = bf16[8,1024,128]{2,1,0:T(8,128)(2,1)} copy-done((bf16[8,1024,128]{2,1,0:T(8,128)(2,1)}, bf16[8,1024,128]{2,1,0:T(8,128)(2,1)S(1)}, u32[]{:S(2)}) %copy-start.6) | copy-done | bytes 2097176
  56.1 0.0 copy-start.9
  56.1 0.7 copy-done.9
  56.8 16.8 %all-to-all-done.1 = bf16[16,2,2,128,128]{4,3,2,1,0:T(8,128)(2,1)} async-done(((bf16[16,2,2,128,128]{4,3,2,1,0:T(8,128)(2,1)}), bf16[16,2,2,128,128]{4,3,2,1,0:T(8,128)(2,1)}, u32[]{:S(2)}, u32[]{:S(2)}) %all-to-all-start.1) | async-done | bytes 2097184 | tf_op jit(solution)/shard_map/all_to_all | solution.py:325
  73.7 12.8 %picks.1 = bf16[256,8192]{1,0:T(8,128)(2,1)} custom-call(s32[16,2]{1,0:T(8,128)} %get-tuple-element.22.slot_ref, bf16[32,2,128,128]{3,2,1,0:T(8,128)(2,1)} %bitcast.2.landed_hbm, bf16[8,1024,128]{2,1,0:T(8,128)(2,1)} %copy-done.5, bf16[8,1024,128]{2,1,0:T(8,128)(2,1)} %copy-done.6, bf16[1024,128]{1,0:T(8,128)(2,1)} %copy-done.9, ...), custom_call_target="tpu_custom_call" | custom-call | flops 8589934592 | bytes 16777216 | tf_op jit(solution)/shard_map/picks/pallas_call | solution.py:354
  (3 shorter events, 0.1 us)
Async XLA Ops:
  0.0 15.3 %collective-permute-start.1 = (bf16[256,1024]{1,0:T(8,128)(2,1)}, bf16[256,1024]{1,0:T(8,128)(2,1)S(1)}, u32[]{:S(2)}, u32[]{:S(2)}) collective-permute-start(bf16[256,1024]{1,0:T(8,128)(2,1)} %v_ref.7), channel_id=1, source_target_pairs={{15,0},{0,1},{1,2},{2,3},{3,4},{4,5},{5,6},{6,7},{7,8},{8,9},{9,10... | collective-permute-start | bytes 1572872 | tf_op jit(solution)/shard_map/ppermute | solution.py:294
  5.4 9.9 %collective-permute-start = (bf16[256,1024]{1,0:T(8,128)(2,1)}, bf16[256,1024]{1,0:T(8,128)(2,1)S(1)}, u32[]{:S(2)}, u32[]{:S(2)}) collective-permute-start(bf16[256,1024]{1,0:T(8,128)(2,1)} %get-tuple-element.24.k_ref), channel_id=1, source_target_pairs={{15,0},{0,1},{1,2},{2,3},{3,4},{4,5},{5,6},{6,7},{7,8},{8,9},{9,10... | collective-permute-start | bytes 1572872 | tf_op jit(solution)/shard_map/ppermute | solution.py:311
  5.5 9.8 %all-to-all-start = ((s32[16,1,2]{2,1,0:T(1,128)}), s32[16,1,2]{2,1,0:T(1,128)S(1)}, u32[]{:S(2)}, u32[]{:S(2)}) async-start(s32[16,1,2]{2,1,0:T(1,128)} %get-tuple-element.23), calls=%async_computation | async-start | bytes 16384 | tf_op jit(solution)/shard_map/all_to_all | solution.py:312
  10.9 29.9 %collective-permute-start.2 = (bf16[128,2048]{1,0:T(8,128)(2,1)}, bf16[128,2048]{1,0:T(8,128)(2,1)}, u32[]{:S(2)}, u32[]{:S(2)}) collective-permute-start(bf16[128,2048]{1,0:T(8,128)(2,1)} %get-tuple-element.30), channel_id=1, source_target_pairs={{14,0},{0,2},{2,4},{4,6},{6,8},{8,10},{10,12},{12,14},{30,16},{16,... | collective-permute-start | bytes 1572872 | tf_op jit(solution)/shard_map/ppermute | solution.py:314
  15.3 0.6 copy-start.11
  19.0 7.2 %copy-start = (bf16[256,1024]{1,0:T(8,128)(2,1)S(1)}, bf16[256,1024]{1,0:T(8,128)(2,1)}, u32[]{:S(2)}) copy-start(bf16[256,1024]{1,0:T(8,128)(2,1)} %v_ref.7) | copy-start | bytes 1572868
  19.0 7.2 %copy-start.1 = (bf16[256,1024]{1,0:T(8,128)(2,1)S(1)}, bf16[256,1024]{1,0:T(8,128)(2,1)}, u32[]{:S(2)}) copy-start(bf16[256,1024]{1,0:T(8,128)(2,1)} %get-tuple-element.24.k_ref) | copy-start | bytes 1572868
  19.0 7.2 %copy-start.3 = (f32[256,128]{1,0:T(8,128)S(1)}, f32[256,128]{1,0:T(8,128)}, u32[]{:S(2)}) copy-start(f32[256,128]{1,0:T(8,128)} %get-tuple-element.26.cos_ref) | copy-start | bytes 393220
  19.0 7.2 %copy-start.4 = (f32[256,128]{1,0:T(8,128)S(1)}, f32[256,128]{1,0:T(8,128)}, u32[]{:S(2)}) copy-start(f32[256,128]{1,0:T(8,128)} %get-tuple-element.27.sin_ref) | copy-start | bytes 393220
  19.0 54.7 %all-to-all-start.1 = ((bf16[16,2,2,128,128]{4,3,2,1,0:T(8,128)(2,1)}), bf16[16,2,2,128,128]{4,3,2,1,0:T(8,128)(2,1)}, u32[]{:S(2)}, u32[]{:S(2)}) async-start(bf16[16,2,2,128,128]{4,3,2,1,0:T(8,128)(2,1)} %gather.1), calls=%async_computation.1 | async-start | bytes 4194304 | tf_op jit(solution)/shard_map/all_to_all | solution.py:325
  26.2 2.2 %copy-start.2 = (bf16[256,8192]{1,0:T(8,128)(2,1)S(1)}, bf16[256,8192]{1,0:T(8,128)(2,1)}, u32[]{:S(2)}) copy-start(bf16[256,8192]{1,0:T(8,128)(2,1)} %q_ref.3) | copy-start | bytes 12582916
  38.2 1.3 %copy-start.8 = (bf16[8,1024,128]{2,1,0:T(8,128)(2,1)}, bf16[8,1024,128]{2,1,0:T(8,128)(2,1)S(1)}, u32[]{:S(2)}) copy-start(bf16[8,1024,128]{2,1,0:T(8,128)(2,1)S(1)} %get-tuple-element.38.rest_4_) | copy-start | bytes 6291460
  39.6 0.7 copy-start.10
  40.3 1.3 %copy-start.7 = (bf16[8,1024,128]{2,1,0:T(8,128)(2,1)}, bf16[8,1024,128]{2,1,0:T(8,128)(2,1)S(1)}, u32[]{:S(2)}) copy-start(bf16[8,1024,128]{2,1,0:T(8,128)(2,1)S(1)} %get-tuple-element.37.rest_3_) | copy-start | bytes 6291460
  40.4 2.0 %collective-permute-start.3 = (bf16[128,2048]{1,0:T(8,128)(2,1)S(1)}, bf16[128,2048]{1,0:T(8,128)(2,1)S(1)}, u32[]{:S(2)}, u32[]{:S(2)}) collective-permute-start(bf16[128,2048]{1,0:T(8,128)(2,1)S(1)} %pad_maximum_fusion), channel_id=1, source_target_pairs={{1,0},{0,1},{3,2},{2,3},{5,4},{4,5},{7,6},{6,7},{9,8},{8,9},{11,10... | collective-permute-start | bytes 1572872 | tf_op jit(solution)/shard_map/ppermute | solution.py:349
  53.4 1.4 %copy-start.5 = (bf16[8,1024,128]{2,1,0:T(8,128)(2,1)}, bf16[8,1024,128]{2,1,0:T(8,128)(2,1)S(1)}, u32[]{:S(2)}) copy-start(bf16[8,1024,128]{2,1,0:T(8,128)(2,1)S(1)} %get-tuple-element.34.rest_0_) | copy-start | bytes 6291460
  54.7 1.4 %copy-start.6 = (bf16[8,1024,128]{2,1,0:T(8,128)(2,1)}, bf16[8,1024,128]{2,1,0:T(8,128)(2,1)S(1)}, u32[]{:S(2)}) copy-start(bf16[8,1024,128]{2,1,0:T(8,128)(2,1)S(1)} %get-tuple-element.35.rest_1_) | copy-start | bytes 6291460
  56.1 0.7 copy-start.9

commit v5 on v4

--- a/solution.py
+++ b/solution.py
@@ -47,9 +47,13 @@
 
 
 def prep_kernel(
-    limit, picks_ref, k_ref, v_ref, pos_ref, freq_ref, kr_ref, last_ref, cos_ref, sin_ref, table_ref, slot_ref, count_ref
+    limit, picks_ref, k_ref, v_hbm, pos_ref, freq_ref, kr_ref, last_ref, cos_ref, sin_ref, table_ref, slot_ref, count_ref, sem
 ):
     shards = table_ref.shape[0]
+    tail = pltpu.make_async_copy(
+        v_hbm.at[pl.ds((BLOCKS - 1) * BLOCK_TOKENS, BLOCK_TOKENS), :], last_ref.at[:, pl.ds(KEY_WIDTH, KEY_WIDTH)], sem
+    )
+    tail.start()
 
     @pl.loop(0, shards)
     def _(i):
@@ -93,7 +97,7 @@
             kr_ref[rows, cols] = rotated
             if b == BLOCKS - 1:
                 last_ref[:, cols] = rotated
-    last_ref[:, KEY_WIDTH:] = v_ref[(BLOCKS - 1) * BLOCK_TOKENS :, :]
+    tail.wait()
 
 
 def gather_kernel(wanted_ref, k_ref, v_ref, out_ref, sems):
@@ -302,9 +306,9 @@
             jax.ShapeDtypeStruct((window, 1, limit), jnp.int32),
             jax.ShapeDtypeStruct((BLOCKS * KEY_VALUE_HEADS, PICKED_BLOCKS), jnp.int32),
         ),
-        in_specs=[smem, vmem, vmem, vmem, vmem],
+        in_specs=[smem, vmem, hbm, vmem, vmem],
         out_specs=(vmem, vmem, vmem, vmem, smem, smem),
-        scratch_shapes=[pltpu.SMEM((window,), jnp.int32)],
+        scratch_shapes=[pltpu.SMEM((window,), jnp.int32), pltpu.SemaphoreType.DMA],
         name="prep",
     )(picks.transpose(0, 2, 1), keys, values, positions.reshape(BLOCKS, BLOCK_TOKENS), jnp.asarray(frequencies()))
 

time: 87.1 us -> 87.1 us (level)
  no operation moved by 1% of the time
where the time goes in v5:
time: 87.1 us; the launch traced here: 86.7 us
  Pallas kernels  40.2 us (46%)
  waiting for transfers between devices  20.7 us (24%)
  starting transfers between devices  16.3 us (19%)
  local copies, waits for them, and re-layouts  9.12 us (10%)
    pallas_call x2, Pallas kernels, band(): pl.pallas_call(functools.partial(band_kernel, b), out_shape=(jax.ShapeDty...  20.9 us
    all_to_all x1, waiting for transfers between devices, shards(): lax.all_to_all(answer, 'ctx', split_axis=0, concat_axis=0, tiled=True)  16.8 us
    pallas_call x1, Pallas kernels, shards(): pl.pallas_call(picks_kernel, out_shape=jax.ShapeDtypeStruct((tokens, QUER...  12.8 us
    unnamed x24, local copies, waits for them, and re-layouts  9.08 us
    all_to_all x1, starting transfers between devices, shards(): lax.all_to_all(answer, 'ctx', split_axis=0, concat_axis=0, tiled=True)  7.12 us
    all_to_all x1, starting transfers between devices, shards(): lax.all_to_all(table, 'ctx', split_axis=0, concat_axis=0, tiled=True)  5.39 us
    pallas_call x1, Pallas kernels, shards(): pl.pallas_call(functools.partial(prep_kernel, limit), out_shape=(jax.Shap...  3.49 us
    pallas_call x1, Pallas kernels, shards(): pl.pallas_call(gather_kernel, out_shape=jax.ShapeDtypeStruct((window, lim...  3.07 us
  transfers between devices with their start and end apart: 6, of which 3 were waited for; matrix products, arithmetic and copies ran while one was open for 0% of the time, Pallas kernels for 32%

profile of v5, /device:TPU:15, one launch (start us, length us, event | category | flops | bytes accessed | tf_op | source)
XLA Modules:
  0.0 86.7 jit_solution(1989861302633459761)
XLA Ops:
  0.0 1.8 %collective-permute-start.1 = (bf16[256,1024]{1,0:T(8,128)(2,1)}, bf16[256,1024]{1,0:T(8,128)(2,1)S(1)}, u32[]{:S(2)}, u32[]{:S(2)}) collective-permute-start(bf16[256,1024]{1,0:T(8,128)(2,1)} %v_ref.5), channel_id=1, source_target_pairs={{15,0},{0,1},{1,2},{2,3},{3,4},{4,5},{5,6},{6,7},{7,8},{8,9},{9,10... | collective-permute-start | bytes 1572872 | tf_op jit(solution)/shard_map/ppermute | solution.py:298
  1.8 3.5 %prep.1 = (bf16[256,1024]{1,0:T(8,128)(2,1)}, bf16[128,2048]{1,0:T(8,128)(2,1)}, f32[256,128]{1,0:T(8,128)}, f32[256,128]{1,0:T(8,128)}, s32[16,1,2]{2,1,0:T(1,128)}, /*index=5*/s32[16,2]{1,0:T(8,128)}) custom-call(s32[2,2,8]{2,1,0:T(2,128)} %bitcast.4, bf16[256,1024]{1,0:T(8,128)(2,1)} %k_ref.1, bf16[256,1024]{1,0:T(8,128)(2,1)} %v_ref.5, ...), custom_call_target="tpu_custom_call" | custom-call | tf_op jit(solution)/shard_map/prep/pallas_call | solution.py:299
  5.3 0.1 collective-permute-start
  5.4 5.4 %all-to-all-start = ((s32[16,1,2]{2,1,0:T(1,128)}), s32[16,1,2]{2,1,0:T(1,128)S(1)}, u32[]{:S(2)}, u32[]{:S(2)}) async-start(s32[16,1,2]{2,1,0:T(1,128)} %get-tuple-element.23), calls=%async_computation | async-start | bytes 16384 | tf_op jit(solution)/shard_map/all_to_all | solution.py:316
  10.8 1.5 %collective-permute-start.2 = (bf16[128,2048]{1,0:T(8,128)(2,1)}, bf16[128,2048]{1,0:T(8,128)(2,1)}, u32[]{:S(2)}, u32[]{:S(2)}) collective-permute-start(bf16[128,2048]{1,0:T(8,128)(2,1)} %get-tuple-element.30), channel_id=1, source_target_pairs={{14,0},{0,2},{2,4},{4,6},{6,8},{8,10},{10,12},{12,14},{30,16},{16,... | collective-permute-start | bytes 1572872 | tf_op jit(solution)/shard_map/ppermute | solution.py:318
  12.2 3.1 %all-to-all-done.wanted_ref = s32[16,1,2]{2,1,0:T(1,128)S(1)} async-done(((s32[16,1,2]{2,1,0:T(1,128)}), s32[16,1,2]{2,1,0:T(1,128)S(1)}, u32[]{:S(2)}, u32[]{:S(2)}) %all-to-all-start) | async-done | bytes 160 | tf_op jit(solution)/shard_map/all_to_all | solution.py:316
  15.3 0.0 copy-start.11
  15.3 0.0 collective-permute-done.1.nv_ref
  15.3 0.0 collective-permute-done.nk_ref
  15.3 0.6 copy-done.11
  15.9 3.1 %gather.1 = bf16[16,2,2,128,128]{4,3,2,1,0:T(8,128)(2,1)} custom-call(s32[16,1,2]{2,1,0:T(1,128)} %copy-done.11, bf16[256,1024]{1,0:T(8,128)(2,1)} %get-tuple-element.24.k_ref, bf16[256,1024]{1,0:T(8,128)(2,1)} %v_ref.5), custom_call_target="tpu_custom_call" | custom-call | bytes 62914560 | tf_op jit(solution)/shard_map/gather/pallas_call | solution.py:320
  19.0 0.0 copy-start
  19.0 0.0 copy-start.1
  19.0 0.0 copy-start.3
  19.0 0.0 copy-start.4
  19.0 7.1 %all-to-all-start.1 = ((bf16[16,2,2,128,128]{4,3,2,1,0:T(8,128)(2,1)}), bf16[16,2,2,128,128]{4,3,2,1,0:T(8,128)(2,1)}, u32[]{:S(2)}, u32[]{:S(2)}) async-start(bf16[16,2,2,128,128]{4,3,2,1,0:T(8,128)(2,1)} %gather.1), calls=%async_computation.1 | async-start | bytes 4194304 | tf_op jit(solution)/shard_map/all_to_all | solution.py:329
  26.1 0.0 copy-done
  26.1 0.0 copy-done.1
  26.2 0.0 copy-done.3
  26.2 0.0 copy-done.4
  26.2 0.0 copy-start.2
  26.2 2.2 %copy-done.2 = bf16[256,8192]{1,0:T(8,128)(2,1)S(1)} copy-done((bf16[256,8192]{1,0:T(8,128)(2,1)S(1)}, bf16[256,8192]{1,0:T(8,128)(2,1)}, u32[]{:S(2)}) %copy-start.2) | copy-done | bytes 4194328
  28.4 9.8 %band.2 = (bf16[8,1024,128]{2,1,0:T(8,128)(2,1)S(1)}, bf16[8,1024,128]{2,1,0:T(8,128)(2,1)S(1)}, bf16[1024,128]{1,0:T(8,128)(2,1)S(1)}) custom-call(s32[1]{0:T(128)} %bitcast.3.me_ref, bf16[256,8192]{1,0:T(8,128)(2,1)S(1)} %copy-done.2, f32[256,128]{1,0:T(8,128)S(1)} %copy-done.3, f32[256,128]{1,0:T(8,128)S(1)} %copy-done.4, ...), custom_call_target="tpu_custom_call" | custom-call | flops 214748364800 | bytes 8388608 | tf_op jit(solution)/shard_map/band/pallas_call | solution.py:336
  38.2 0.0 copy-start.8
  38.2 1.3 %copy-done.8 = bf16[8,1024,128]{2,1,0:T(8,128)(2,1)} copy-done((bf16[8,1024,128]{2,1,0:T(8,128)(2,1)}, bf16[8,1024,128]{2,1,0:T(8,128)(2,1)S(1)}, u32[]{:S(2)}) %copy-start.8) | copy-done | bytes 2097176
  39.6 0.0 copy-start.10
  39.6 0.7 copy-done.10
  40.3 0.0 copy-start.7
  40.4 0.4 collective-permute-start.3
  40.8 0.0 collective-permute-done.2.rest_0_
  40.8 0.8 copy-done.7
  41.6 0.8 collective-permute-done.3.rest_1_
  42.3 11.0 %band.3 = (bf16[8,1024,128]{2,1,0:T(8,128)(2,1)S(1)}, bf16[8,1024,128]{2,1,0:T(8,128)(2,1)S(1)}, bf16[1024,128]{1,0:T(8,128)(2,1)S(1)}) custom-call(s32[1]{0:T(128)} %bitcast.3.me_ref, bf16[256,8192]{1,0:T(8,128)(2,1)S(1)} %copy-done.2, f32[256,128]{1,0:T(8,128)S(1)} %copy-done.3, f32[256,128]{1,0:T(8,128)S(1)} %copy-done.4, ...), custom_call_target="tpu_custom_call" | custom-call | flops 4294967296 | bytes 8388608 | tf_op jit(solution)/shard_map/band/pallas_call | solution.py:336
  53.4 0.0 copy-start.5
  53.4 1.4 %copy-done.5 = bf16[8,1024,128]{2,1,0:T(8,128)(2,1)} copy-done((bf16[8,1024,128]{2,1,0:T(8,128)(2,1)}, bf16[8,1024,128]{2,1,0:T(8,128)(2,1)S(1)}, u32[]{:S(2)}) %copy-start.5) | copy-done | bytes 2097176
  54.7 0.0 copy-start.6
  54.7 1.4 %copy-done.6 = bf16[8,1024,128]{2,1,0:T(8,128)(2,1)} copy-done((bf16[8,1024,128]{2,1,0:T(8,128)(2,1)}, bf16[8,1024,128]{2,1,0:T(8,128)(2,1)S(1)}, u32[]{:S(2)}) %copy-start.6) | copy-done | bytes 2097176
  56.1 0.0 copy-start.9
  56.1 0.7 copy-done.9
  56.8 16.8 %all-to-all-done.1 = bf16[16,2,2,128,128]{4,3,2,1,0:T(8,128)(2,1)} async-done(((bf16[16,2,2,128,128]{4,3,2,1,0:T(8,128)(2,1)}), bf16[16,2,2,128,128]{4,3,2,1,0:T(8,128)(2,1)}, u32[]{:S(2)}, u32[]{:S(2)}) %all-to-all-start.1) | async-done | bytes 2097184 | tf_op jit(solution)/shard_map/all_to_all | solution.py:329
  73.7 12.8 %picks.1 = bf16[256,8192]{1,0:T(8,128)(2,1)} custom-call(s32[16,2]{1,0:T(8,128)} %get-tuple-element.22.slot_ref, bf16[32,2,128,128]{3,2,1,0:T(8,128)(2,1)} %bitcast.2.landed_hbm, bf16[8,1024,128]{2,1,0:T(8,128)(2,1)} %copy-done.5, bf16[8,1024,128]{2,1,0:T(8,128)(2,1)} %copy-done.6, bf16[1024,128]{1,0:T(8,128)(2,1)} %copy-done.9, ...), custom_call_target="tpu_custom_call" | custom-call | flops 8589934592 | bytes 16777216 | tf_op jit(solution)/shard_map/picks/pallas_call | solution.py:358
  (3 shorter events, 0.1 us)
Async XLA Ops:
  0.0 15.3 %collective-permute-start.1 = (bf16[256,1024]{1,0:T(8,128)(2,1)}, bf16[256,1024]{1,0:T(8,128)(2,1)S(1)}, u32[]{:S(2)}, u32[]{:S(2)}) collective-permute-start(bf16[256,1024]{1,0:T(8,128)(2,1)} %v_ref.5), channel_id=1, source_target_pairs={{15,0},{0,1},{1,2},{2,3},{3,4},{4,5},{5,6},{6,7},{7,8},{8,9},{9,10... | collective-permute-start | bytes 1572872 | tf_op jit(solution)/shard_map/ppermute | solution.py:298
  5.3 10.0 %collective-permute-start = (bf16[256,1024]{1,0:T(8,128)(2,1)}, bf16[256,1024]{1,0:T(8,128)(2,1)S(1)}, u32[]{:S(2)}, u32[]{:S(2)}) collective-permute-start(bf16[256,1024]{1,0:T(8,128)(2,1)} %get-tuple-element.24.k_ref), channel_id=1, source_target_pairs={{15,0},{0,1},{1,2},{2,3},{3,4},{4,5},{5,6},{6,7},{7,8},{8,9},{9,10... | collective-permute-start | bytes 1572872 | tf_op jit(solution)/shard_map/ppermute | solution.py:315
  5.4 9.9 %all-to-all-start = ((s32[16,1,2]{2,1,0:T(1,128)}), s32[16,1,2]{2,1,0:T(1,128)S(1)}, u32[]{:S(2)}, u32[]{:S(2)}) async-start(s32[16,1,2]{2,1,0:T(1,128)} %get-tuple-element.23), calls=%async_computation | async-start | bytes 16384 | tf_op jit(solution)/shard_map/all_to_all | solution.py:316
  10.8 30.0 %collective-permute-start.2 = (bf16[128,2048]{1,0:T(8,128)(2,1)}, bf16[128,2048]{1,0:T(8,128)(2,1)}, u32[]{:S(2)}, u32[]{:S(2)}) collective-permute-start(bf16[128,2048]{1,0:T(8,128)(2,1)} %get-tuple-element.30), channel_id=1, source_target_pairs={{14,0},{0,2},{2,4},{4,6},{6,8},{8,10},{10,12},{12,14},{30,16},{16,... | collective-permute-start | bytes 1572872 | tf_op jit(solution)/shard_map/ppermute | solution.py:318
  15.3 0.6 copy-start.11
  19.0 7.2 %copy-start = (bf16[256,1024]{1,0:T(8,128)(2,1)S(1)}, bf16[256,1024]{1,0:T(8,128)(2,1)}, u32[]{:S(2)}) copy-start(bf16[256,1024]{1,0:T(8,128)(2,1)} %v_ref.5) | copy-start | bytes 1572868
  19.0 7.2 %copy-start.1 = (bf16[256,1024]{1,0:T(8,128)(2,1)S(1)}, bf16[256,1024]{1,0:T(8,128)(2,1)}, u32[]{:S(2)}) copy-start(bf16[256,1024]{1,0:T(8,128)(2,1)} %get-tuple-element.24.k_ref) | copy-start | bytes 1572868
  19.0 7.2 %copy-start.3 = (f32[256,128]{1,0:T(8,128)S(1)}, f32[256,128]{1,0:T(8,128)}, u32[]{:S(2)}) copy-start(f32[256,128]{1,0:T(8,128)} %get-tuple-element.26.cos_ref) | copy-start | bytes 393220
  19.0 7.2 %copy-start.4 = (f32[256,128]{1,0:T(8,128)S(1)}, f32[256,128]{1,0:T(8,128)}, u32[]{:S(2)}) copy-start(f32[256,128]{1,0:T(8,128)} %get-tuple-element.27.sin_ref) | copy-start | bytes 393220
  19.0 54.7 %all-to-all-start.1 = ((bf16[16,2,2,128,128]{4,3,2,1,0:T(8,128)(2,1)}), bf16[16,2,2,128,128]{4,3,2,1,0:T(8,128)(2,1)}, u32[]{:S(2)}, u32[]{:S(2)}) async-start(bf16[16,2,2,128,128]{4,3,2,1,0:T(8,128)(2,1)} %gather.1), calls=%async_computation.1 | async-start | bytes 4194304 | tf_op jit(solution)/shard_map/all_to_all | solution.py:329
  26.2 2.2 %copy-start.2 = (bf16[256,8192]{1,0:T(8,128)(2,1)S(1)}, bf16[256,8192]{1,0:T(8,128)(2,1)}, u32[]{:S(2)}) copy-start(bf16[256,8192]{1,0:T(8,128)(2,1)} %q_ref.3) | copy-start | bytes 12582916
  38.2 1.3 %copy-start.8 = (bf16[8,1024,128]{2,1,0:T(8,128)(2,1)}, bf16[8,1024,128]{2,1,0:T(8,128)(2,1)S(1)}, u32[]{:S(2)}) copy-start(bf16[8,1024,128]{2,1,0:T(8,128)(2,1)S(1)} %get-tuple-element.38.rest_4_) | copy-start | bytes 6291460
  39.6 0.7 copy-start.10
  40.3 1.3 %copy-start.7 = (bf16[8,1024,128]{2,1,0:T(8,128)(2,1)}, bf16[8,1024,128]{2,1,0:T(8,128)(2,1)S(1)}, u32[]{:S(2)}) copy-start(bf16[8,1024,128]{2,1,0:T(8,128)(2,1)S(1)} %get-tuple-element.37.rest_3_) | copy-start | bytes 6291460
  40.4 2.0 %collective-permute-start.3 = (bf16[128,2048]{1,0:T(8,128)(2,1)S(1)}, bf16[128,2048]{1,0:T(8,128)(2,1)S(1)}, u32[]{:S(2)}, u32[]{:S(2)}) collective-permute-start(bf16[128,2048]{1,0:T(8,128)(2,1)S(1)} %pad_maximum_fusion), channel_id=1, source_target_pairs={{1,0},{0,1},{3,2},{2,3},{5,4},{4,5},{7,6},{6,7},{9,8},{8,9},{11,10... | collective-permute-start | bytes 1572872 | tf_op jit(solution)/shard_map/ppermute | solution.py:353
  53.4 1.4 %copy-start.5 = (bf16[8,1024,128]{2,1,0:T(8,128)(2,1)}, bf16[8,1024,128]{2,1,0:T(8,128)(2,1)S(1)}, u32[]{:S(2)}) copy-start(bf16[8,1024,128]{2,1,0:T(8,128)(2,1)S(1)} %get-tuple-element.34.rest_0_) | copy-start | bytes 6291460
  54.7 1.4 %copy-start.6 = (bf16[8,1024,128]{2,1,0:T(8,128)(2,1)}, bf16[8,1024,128]{2,1,0:T(8,128)(2,1)S(1)}, u32[]{:S(2)}) copy-start(bf16[8,1024,128]{2,1,0:T(8,128)(2,1)S(1)} %get-tuple-element.35.rest_1_) | copy-start | bytes 6291460
  56.1 0.7 copy-start.9

commit v6 on v5

--- a/solution.py
+++ b/solution.py
@@ -27,7 +27,7 @@
 PARTS = 3
 
 BAND_ROWS = 256
-PICK_ROWS = 512
+PICK_ROWS = 256
 PICK_UNROLL = 8
 PICK_AHEAD = 1
 

time: 87.1 us -> 87.2 us (level)
  no operation moved by 1% of the time
where the time goes in v6:
time: 87.2 us; the launch traced here: 86.7 us
  Pallas kernels  40.3 us (46%)
  waiting for transfers between devices  20.7 us (24%)
  starting transfers between devices  16.3 us (19%)
  local copies, waits for them, and re-layouts  9.12 us (10%)
    pallas_call x2, Pallas kernels, band(): pl.pallas_call(functools.partial(band_kernel, b), out_shape=(jax.ShapeDty...  20.9 us
    all_to_all x1, waiting for transfers between devices, shards(): lax.all_to_all(answer, 'ctx', split_axis=0, concat_axis=0, tiled=True)  16.8 us
    pallas_call x1, Pallas kernels, shards(): pl.pallas_call(picks_kernel, out_shape=jax.ShapeDtypeStruct((tokens, QUER...  12.9 us
    unnamed x24, local copies, waits for them, and re-layouts  9.08 us
    all_to_all x1, starting transfers between devices, shards(): lax.all_to_all(answer, 'ctx', split_axis=0, concat_axis=0, tiled=True)  7.12 us
    all_to_all x1, starting transfers between devices, shards(): lax.all_to_all(table, 'ctx', split_axis=0, concat_axis=0, tiled=True)  5.39 us
    pallas_call x1, Pallas kernels, shards(): pl.pallas_call(functools.partial(prep_kernel, limit), out_shape=(jax.Shap...  3.49 us
    pallas_call x1, Pallas kernels, shards(): pl.pallas_call(gather_kernel, out_shape=jax.ShapeDtypeStruct((window, lim...  3.07 us
  transfers between devices with their start and end apart: 6, of which 3 were waited for; matrix products, arithmetic and copies ran while one was open for 0% of the time, Pallas kernels for 32%

profile of v6, /device:TPU:15, one launch (start us, length us, event | category | flops | bytes accessed | tf_op | source)
XLA Modules:
  0.0 86.7 jit_solution(468139978881139766)
XLA Ops:
  0.0 1.8 %collective-permute-start.1 = (bf16[256,1024]{1,0:T(8,128)(2,1)}, bf16[256,1024]{1,0:T(8,128)(2,1)S(1)}, u32[]{:S(2)}, u32[]{:S(2)}) collective-permute-start(bf16[256,1024]{1,0:T(8,128)(2,1)} %v_ref.5), channel_id=1, source_target_pairs={{15,0},{0,1},{1,2},{2,3},{3,4},{4,5},{5,6},{6,7},{7,8},{8,9},{9,10... | collective-permute-start | bytes 1572872 | tf_op jit(solution)/shard_map/ppermute | solution.py:298
  1.8 3.5 %prep.1 = (bf16[256,1024]{1,0:T(8,128)(2,1)}, bf16[128,2048]{1,0:T(8,128)(2,1)}, f32[256,128]{1,0:T(8,128)}, f32[256,128]{1,0:T(8,128)}, s32[16,1,2]{2,1,0:T(1,128)}, /*index=5*/s32[16,2]{1,0:T(8,128)}) custom-call(s32[2,2,8]{2,1,0:T(2,128)} %bitcast.4, bf16[256,1024]{1,0:T(8,128)(2,1)} %k_ref.1, bf16[256,1024]{1,0:T(8,128)(2,1)} %v_ref.5, ...), custom_call_target="tpu_custom_call" | custom-call | tf_op jit(solution)/shard_map/prep/pallas_call | solution.py:299
  5.3 0.1 collective-permute-start
  5.4 5.4 %all-to-all-start = ((s32[16,1,2]{2,1,0:T(1,128)}), s32[16,1,2]{2,1,0:T(1,128)S(1)}, u32[]{:S(2)}, u32[]{:S(2)}) async-start(s32[16,1,2]{2,1,0:T(1,128)} %get-tuple-element.23), calls=%async_computation | async-start | bytes 16384 | tf_op jit(solution)/shard_map/all_to_all | solution.py:316
  10.8 1.5 %collective-permute-start.2 = (bf16[128,2048]{1,0:T(8,128)(2,1)}, bf16[128,2048]{1,0:T(8,128)(2,1)}, u32[]{:S(2)}, u32[]{:S(2)}) collective-permute-start(bf16[128,2048]{1,0:T(8,128)(2,1)} %get-tuple-element.30), channel_id=1, source_target_pairs={{14,0},{0,2},{2,4},{4,6},{6,8},{8,10},{10,12},{12,14},{30,16},{16,... | collective-permute-start | bytes 1572872 | tf_op jit(solution)/shard_map/ppermute | solution.py:318
  12.2 3.1 %all-to-all-done.wanted_ref = s32[16,1,2]{2,1,0:T(1,128)S(1)} async-done(((s32[16,1,2]{2,1,0:T(1,128)}), s32[16,1,2]{2,1,0:T(1,128)S(1)}, u32[]{:S(2)}, u32[]{:S(2)}) %all-to-all-start) | async-done | bytes 160 | tf_op jit(solution)/shard_map/all_to_all | solution.py:316
  15.3 0.0 copy-start.11
  15.3 0.0 collective-permute-done.1.nv_ref
  15.3 0.0 collective-permute-done.nk_ref
  15.3 0.6 copy-done.11
  15.9 3.1 %gather.1 = bf16[16,2,2,128,128]{4,3,2,1,0:T(8,128)(2,1)} custom-call(s32[16,1,2]{2,1,0:T(1,128)} %copy-done.11, bf16[256,1024]{1,0:T(8,128)(2,1)} %get-tuple-element.24.k_ref, bf16[256,1024]{1,0:T(8,128)(2,1)} %v_ref.5), custom_call_target="tpu_custom_call" | custom-call | bytes 62914560 | tf_op jit(solution)/shard_map/gather/pallas_call | solution.py:320
  19.0 0.0 copy-start
  19.0 0.0 copy-start.1
  19.0 0.0 copy-start.3
  19.0 0.0 copy-start.4
  19.0 7.1 %all-to-all-start.1 = ((bf16[16,2,2,128,128]{4,3,2,1,0:T(8,128)(2,1)}), bf16[16,2,2,128,128]{4,3,2,1,0:T(8,128)(2,1)}, u32[]{:S(2)}, u32[]{:S(2)}) async-start(bf16[16,2,2,128,128]{4,3,2,1,0:T(8,128)(2,1)} %gather.1), calls=%async_computation.1 | async-start | bytes 4194304 | tf_op jit(solution)/shard_map/all_to_all | solution.py:329
  26.1 0.0 copy-done
  26.1 0.0 copy-done.1
  26.2 0.0 copy-done.3
  26.2 0.0 copy-done.4
  26.2 0.0 copy-start.2
  26.2 2.2 %copy-done.2 = bf16[256,8192]{1,0:T(8,128)(2,1)S(1)} copy-done((bf16[256,8192]{1,0:T(8,128)(2,1)S(1)}, bf16[256,8192]{1,0:T(8,128)(2,1)}, u32[]{:S(2)}) %copy-start.2) | copy-done | bytes 4194328
  28.4 9.8 %band.2 = (bf16[8,1024,128]{2,1,0:T(8,128)(2,1)S(1)}, bf16[8,1024,128]{2,1,0:T(8,128)(2,1)S(1)}, bf16[1024,128]{1,0:T(8,128)(2,1)S(1)}) custom-call(s32[1]{0:T(128)} %bitcast.3.me_ref, bf16[256,8192]{1,0:T(8,128)(2,1)S(1)} %copy-done.2, f32[256,128]{1,0:T(8,128)S(1)} %copy-done.3, f32[256,128]{1,0:T(8,128)S(1)} %copy-done.4, ...), custom_call_target="tpu_custom_call" | custom-call | flops 214748364800 | bytes 8388608 | tf_op jit(solution)/shard_map/band/pallas_call | solution.py:336
  38.2 0.0 copy-start.8
  38.2 1.3 %copy-done.8 = bf16[8,1024,128]{2,1,0:T(8,128)(2,1)} copy-done((bf16[8,1024,128]{2,1,0:T(8,128)(2,1)}, bf16[8,1024,128]{2,1,0:T(8,128)(2,1)S(1)}, u32[]{:S(2)}) %copy-start.8) | copy-done | bytes 2097176
  39.6 0.0 copy-start.10
  39.6 0.7 copy-done.10
  40.3 0.0 copy-start.7
  40.4 0.4 collective-permute-start.3
  40.8 0.0 collective-permute-done.2.rest_0_
  40.8 0.8 copy-done.7
  41.6 0.8 collective-permute-done.3.rest_1_
  42.3 11.0 %band.3 = (bf16[8,1024,128]{2,1,0:T(8,128)(2,1)S(1)}, bf16[8,1024,128]{2,1,0:T(8,128)(2,1)S(1)}, bf16[1024,128]{1,0:T(8,128)(2,1)S(1)}) custom-call(s32[1]{0:T(128)} %bitcast.3.me_ref, bf16[256,8192]{1,0:T(8,128)(2,1)S(1)} %copy-done.2, f32[256,128]{1,0:T(8,128)S(1)} %copy-done.3, f32[256,128]{1,0:T(8,128)S(1)} %copy-done.4, ...), custom_call_target="tpu_custom_call" | custom-call | flops 4294967296 | bytes 8388608 | tf_op jit(solution)/shard_map/band/pallas_call | solution.py:336
  53.4 0.0 copy-start.5
  53.4 1.4 %copy-done.5 = bf16[8,1024,128]{2,1,0:T(8,128)(2,1)} copy-done((bf16[8,1024,128]{2,1,0:T(8,128)(2,1)}, bf16[8,1024,128]{2,1,0:T(8,128)(2,1)S(1)}, u32[]{:S(2)}) %copy-start.5) | copy-done | bytes 2097176
  54.7 0.0 copy-start.6
  54.7 1.4 %copy-done.6 = bf16[8,1024,128]{2,1,0:T(8,128)(2,1)} copy-done((bf16[8,1024,128]{2,1,0:T(8,128)(2,1)}, bf16[8,1024,128]{2,1,0:T(8,128)(2,1)S(1)}, u32[]{:S(2)}) %copy-start.6) | copy-done | bytes 2097176
  56.1 0.0 copy-start.9
  56.1 0.7 copy-done.9
  56.8 16.8 %all-to-all-done.1 = bf16[16,2,2,128,128]{4,3,2,1,0:T(8,128)(2,1)} async-done(((bf16[16,2,2,128,128]{4,3,2,1,0:T(8,128)(2,1)}), bf16[16,2,2,128,128]{4,3,2,1,0:T(8,128)(2,1)}, u32[]{:S(2)}, u32[]{:S(2)}) %all-to-all-start.1) | async-done | bytes 2097184 | tf_op jit(solution)/shard_map/all_to_all | solution.py:329
  73.7 12.9 %picks.1 = bf16[256,8192]{1,0:T(8,128)(2,1)} custom-call(s32[16,2]{1,0:T(8,128)} %get-tuple-element.22.slot_ref, bf16[32,2,128,128]{3,2,1,0:T(8,128)(2,1)} %bitcast.2.landed_hbm, bf16[8,1024,128]{2,1,0:T(8,128)(2,1)} %copy-done.5, bf16[8,1024,128]{2,1,0:T(8,128)(2,1)} %copy-done.6, bf16[1024,128]{1,0:T(8,128)(2,1)} %copy-done.9, ...), custom_call_target="tpu_custom_call" | custom-call | flops 8589934592 | bytes 16777216 | tf_op jit(solution)/shard_map/picks/pallas_call | solution.py:358
  (3 shorter events, 0.1 us)
Async XLA Ops:
  0.0 15.3 %collective-permute-start.1 = (bf16[256,1024]{1,0:T(8,128)(2,1)}, bf16[256,1024]{1,0:T(8,128)(2,1)S(1)}, u32[]{:S(2)}, u32[]{:S(2)}) collective-permute-start(bf16[256,1024]{1,0:T(8,128)(2,1)} %v_ref.5), channel_id=1, source_target_pairs={{15,0},{0,1},{1,2},{2,3},{3,4},{4,5},{5,6},{6,7},{7,8},{8,9},{9,10... | collective-permute-start | bytes 1572872 | tf_op jit(solution)/shard_map/ppermute | solution.py:298
  5.3 10.0 %collective-permute-start = (bf16[256,1024]{1,0:T(8,128)(2,1)}, bf16[256,1024]{1,0:T(8,128)(2,1)S(1)}, u32[]{:S(2)}, u32[]{:S(2)}) collective-permute-start(bf16[256,1024]{1,0:T(8,128)(2,1)} %get-tuple-element.24.k_ref), channel_id=1, source_target_pairs={{15,0},{0,1},{1,2},{2,3},{3,4},{4,5},{5,6},{6,7},{7,8},{8,9},{9,10... | collective-permute-start | bytes 1572872 | tf_op jit(solution)/shard_map/ppermute | solution.py:315
  5.4 9.9 %all-to-all-start = ((s32[16,1,2]{2,1,0:T(1,128)}), s32[16,1,2]{2,1,0:T(1,128)S(1)}, u32[]{:S(2)}, u32[]{:S(2)}) async-start(s32[16,1,2]{2,1,0:T(1,128)} %get-tuple-element.23), calls=%async_computation | async-start | bytes 16384 | tf_op jit(solution)/shard_map/all_to_all | solution.py:316
  10.8 30.0 %collective-permute-start.2 = (bf16[128,2048]{1,0:T(8,128)(2,1)}, bf16[128,2048]{1,0:T(8,128)(2,1)}, u32[]{:S(2)}, u32[]{:S(2)}) collective-permute-start(bf16[128,2048]{1,0:T(8,128)(2,1)} %get-tuple-element.30), channel_id=1, source_target_pairs={{14,0},{0,2},{2,4},{4,6},{6,8},{8,10},{10,12},{12,14},{30,16},{16,... | collective-permute-start | bytes 1572872 | tf_op jit(solution)/shard_map/ppermute | solution.py:318
  15.3 0.6 copy-start.11
  19.0 7.2 %copy-start = (bf16[256,1024]{1,0:T(8,128)(2,1)S(1)}, bf16[256,1024]{1,0:T(8,128)(2,1)}, u32[]{:S(2)}) copy-start(bf16[256,1024]{1,0:T(8,128)(2,1)} %v_ref.5) | copy-start | bytes 1572868
  19.0 7.2 %copy-start.1 = (bf16[256,1024]{1,0:T(8,128)(2,1)S(1)}, bf16[256,1024]{1,0:T(8,128)(2,1)}, u32[]{:S(2)}) copy-start(bf16[256,1024]{1,0:T(8,128)(2,1)} %get-tuple-element.24.k_ref) | copy-start | bytes 1572868
  19.0 7.2 %copy-start.3 = (f32[256,128]{1,0:T(8,128)S(1)}, f32[256,128]{1,0:T(8,128)}, u32[]{:S(2)}) copy-start(f32[256,128]{1,0:T(8,128)} %get-tuple-element.26.cos_ref) | copy-start | bytes 393220
  19.0 7.2 %copy-start.4 = (f32[256,128]{1,0:T(8,128)S(1)}, f32[256,128]{1,0:T(8,128)}, u32[]{:S(2)}) copy-start(f32[256,128]{1,0:T(8,128)} %get-tuple-element.27.sin_ref) | copy-start | bytes 393220
  19.0 54.7 %all-to-all-start.1 = ((bf16[16,2,2,128,128]{4,3,2,1,0:T(8,128)(2,1)}), bf16[16,2,2,128,128]{4,3,2,1,0:T(8,128)(2,1)}, u32[]{:S(2)}, u32[]{:S(2)}) async-start(bf16[16,2,2,128,128]{4,3,2,1,0:T(8,128)(2,1)} %gather.1), calls=%async_computation.1 | async-start | bytes 4194304 | tf_op jit(solution)/shard_map/all_to_all | solution.py:329
  26.2 2.2 %copy-start.2 = (bf16[256,8192]{1,0:T(8,128)(2,1)S(1)}, bf16[256,8192]{1,0:T(8,128)(2,1)}, u32[]{:S(2)}) copy-start(bf16[256,8192]{1,0:T(8,128)(2,1)} %q_ref.3) | copy-start | bytes 12582916
  38.2 1.3 %copy-start.8 = (bf16[8,1024,128]{2,1,0:T(8,128)(2,1)}, bf16[8,1024,128]{2,1,0:T(8,128)(2,1)S(1)}, u32[]{:S(2)}) copy-start(bf16[8,1024,128]{2,1,0:T(8,128)(2,1)S(1)} %get-tuple-element.38.rest_4_) | copy-start | bytes 6291460
  39.6 0.7 copy-start.10
  40.3 1.3 %copy-start.7 = (bf16[8,1024,128]{2,1,0:T(8,128)(2,1)}, bf16[8,1024,128]{2,1,0:T(8,128)(2,1)S(1)}, u32[]{:S(2)}) copy-start(bf16[8,1024,128]{2,1,0:T(8,128)(2,1)S(1)} %get-tuple-element.37.rest_3_) | copy-start | bytes 6291460
  40.4 2.0 %collective-permute-start.3 = (bf16[128,2048]{1,0:T(8,128)(2,1)S(1)}, bf16[128,2048]{1,0:T(8,128)(2,1)S(1)}, u32[]{:S(2)}, u32[]{:S(2)}) collective-permute-start(bf16[128,2048]{1,0:T(8,128)(2,1)S(1)} %pad_maximum_fusion), channel_id=1, source_target_pairs={{1,0},{0,1},{3,2},{2,3},{5,4},{4,5},{7,6},{6,7},{9,8},{8,9},{11,10... | collective-permute-start | bytes 1572872 | tf_op jit(solution)/shard_map/ppermute | solution.py:353
  53.4 1.4 %copy-start.5 = (bf16[8,1024,128]{2,1,0:T(8,128)(2,1)}, bf16[8,1024,128]{2,1,0:T(8,128)(2,1)S(1)}, u32[]{:S(2)}) copy-start(bf16[8,1024,128]{2,1,0:T(8,128)(2,1)S(1)} %get-tuple-element.34.rest_0_) | copy-start | bytes 6291460
  54.7 1.4 %copy-start.6 = (bf16[8,1024,128]{2,1,0:T(8,128)(2,1)}, bf16[8,1024,128]{2,1,0:T(8,128)(2,1)S(1)}, u32[]{:S(2)}) copy-start(bf16[8,1024,128]{2,1,0:T(8,128)(2,1)S(1)} %get-tuple-element.35.rest_1_) | copy-start | bytes 6291460
  56.1 0.7 copy-start.9
